TPU v7x, 128 devices: a whole 4x4x4 slice. The times are simulated.
128 devices in a mesh: island: 8 (over z, x_lo), fsdp: 16 (over x_hi, y, core).
Axes of the slice: x: 4 (x_hi: 2, x_lo: 2; x = x_hi * 2 + x_lo), y: 4, z: 4, core: 2. Of those that a mesh axis runs over, the one named last changes fastest.
Arguments:
- tokens: bfloat16 [8, 8192, 8192], P('island', 'fsdp'), may hold values from -6 to 6
- key_grad_out: bfloat16 [8, 8192, 1024], P('island', 'fsdp'), may hold values from -0.0625 to 0.0625
- key_master: float32 [8, 8192, 1024], P('island', 'fsdp'), may hold values from -0.0625 to 0.0625
- key_first: float32 [8, 8192, 1024], P('island', 'fsdp'), may hold values from -4 to 4
- key_second: float32 [8, 8192, 1024], P('island', 'fsdp'), may hold values from 0.05 to 2
- frag_local: float32 [8, 8192, 1024], P('island', 'fsdp'), may hold values from -1.5 to 1.5
- frag_anchor: float32 [8192, 1024], P('fsdp'), may hold values from -1.5 to 1.5
- frag_momentum: float32 [8192, 1024], P('fsdp'), may hold values from -1.5 to 1.5
Outputs:
- new_master: float32 [8, 8192, 1024], P('island', 'fsdp')
- new_first: float32 [8, 8192, 1024], P('island', 'fsdp')
- new_second: float32 [8, 8192, 1024], P('island', 'fsdp')
- next_keys: float32 [8, 8192, 1024], P('island', 'fsdp')
- new_anchor: float32 [8192, 1024], P('fsdp')
- new_momentum: float32 [8192, 1024], P('fsdp')
All inputs are finite; a program needn't handle non-finite values.
Results may differ from a plain program's by a relative error of at most 0.0029.
Values may be sent and summed in bfloat16 or wider, within the bound.
No kernel may reach another device: no remote copies, remote signals or barrier semaphores. Data moves between devices by JAX's collectives and lax.ppermute only.
A program may use at most 192 MiB of HBM per device.

v0:
```python
import jax
import jax.numpy as jnp
from jax import lax
from jax.sharding import PartitionSpec as P

BETA_ONE = 0.9
BETA_TWO = 0.95
INNER_RATE = 0.002
DECAY_RATE = 0.1
EPSILON = 1e-08
OUTER_RATE = 0.7
OUTER_MOMENT = 0.9


def outer_update(outer_grad, anchor_rows, momentum_rows):
    momentum_new = OUTER_MOMENT * momentum_rows + outer_grad
    anchor_new = anchor_rows - OUTER_RATE * (outer_grad + OUTER_MOMENT * momentum_new)
    return (anchor_new, momentum_new)


def per_device(
    tokens, key_grad_out, key_master, key_first, key_second, frag_local, frag_anchor, frag_momentum
):
    activations = tokens[0]
    upstream = key_grad_out[0]
    master = key_master[0]
    feature_slab = activations
    grad = lax.psum_scatter(
        lax.dot_general(
            feature_slab, upstream, (((0,), (0,)), ((), ())), preferred_element_type=jnp.float32
        ),
        "fsdp",
        scatter_dimension=0,
        tiled=True,
    )
    first_new = BETA_ONE * key_first[0] + (1.0 - BETA_ONE) * grad
    second_new = BETA_TWO * key_second[0] + (1.0 - BETA_TWO) * grad * grad
    update = first_new / (jnp.sqrt(second_new) + EPSILON)
    master_new = master - INNER_RATE * (update + DECAY_RATE * master)
    weight_bf = master_new.astype(jnp.bfloat16)
    feature_slab = activations
    key_values = jnp.dot(
        feature_slab,
        lax.all_gather(weight_bf, "fsdp", axis=0, tiled=True),
        preferred_element_type=jnp.float32,
    )
    island_count = lax.axis_size("island")
    pseudo = frag_anchor - frag_local[0]
    summed = lax.psum(pseudo, "island")
    new_anchor, new_momentum = outer_update(summed / island_count, frag_anchor, frag_momentum)
    return (
        master_new[None],
        first_new[None],
        second_new[None],
        key_values[None],
        new_anchor,
        new_momentum,
    )


def solution(mesh):
    return jax.shard_map(
        per_device,
        mesh=mesh,
        in_specs=(
            P("island", "fsdp", None),
            P("island", "fsdp", None),
            P("island", "fsdp", None),
            P("island", "fsdp", None),
            P("island", "fsdp", None),
            P("island", "fsdp", None),
            P("fsdp", None),
            P("fsdp", None),
        ),
        out_specs=(
            P("island", "fsdp", None),
            P("island", "fsdp", None),
            P("island", "fsdp", None),
            P("island", "fsdp", None),
            P("fsdp", None),
            P("fsdp", None),
        ),
        check_vma=False,
    )
```

profile of v0, /device:TPU:1, one launch (start us, length us, event | category | flops | bytes accessed | tf_op | source)
XLA Modules:
  0.0 440.7 jit_solution(17716569214304781898)
XLA Ops:
  8.0 0.0 copy-start
  8.0 0.0 reduce-scatter.2.cloned.1.call-start
  8.1 1.2 copy-done
  9.2 18.7 %fusion.2 = f32[8192,1024]{1,0:T(8,128)} fusion(bf16[1,512,8192]{2,1,0:T(8,128)(2,1)} %param.8, bf16[1,512,1024]{2,1,0:T(8,128)(2,1)S(1)} %copy-done), kind=kOutput, calls=%fused_computation.2 | convolution fusion | flops 8589934592 | bytes 42991616 | tf_op jit(solution)/shard_map/dot_general | solution.py:29
  28.0 0.0 copy-start.2
  28.0 0.0 reduce-scatter.2.cloned.1.call-update
  28.0 0.0 all-reduce.2.cloned.1.call-start
  28.0 1.5 copy-done.2
  29.6 3.5 bitcast_subtract_fusion
  33.0 0.0 all-reduce.2.cloned.1.call-update
  33.0 0.2 all-gather.2.cloned.1.call-start
  33.3 260.7 %reduce-scatter.2.cloned.1.call-done = f32[512,1024]{1,0:T(8,128)} async-done(((f32[8192,1024]{1,0:T(8,128)}), f32[512,1024]{1,0:T(8,128)}) %reduce-scatter.2.cloned.1.call-update) | async-done | bytes 2097168 | tf_op jit(solution)/shard_map/reduce_scatter | solution.py:28
  294.0 8.3 %fusion.13 = (bf16[512,1024]{1,0:T(8,128)(2,1)}, f32[512,1024]{1,0:T(8,128)}, f32[1,512,1024]{2,1,0:T(8,128)}, f32[1,512,1024]{2,1,0:T(8,128)}) fusion(f32[512,1024]{1,0:T(8,128)} %reduce-scatter.2.cloned.1.call-done, f32[1,512,1024]{2,1,0:T(8,128)} %param.12, f32[1,512,1024]{2,1,0:T(8,128)} %param.11, f32[1,512,1024]{2,1,0:T(8,128)} %param.10), kind=kLoop, calls=%fused_computation.18 | loop fusion | flops 7340032 | bytes 15728640 | tf_op jit(solution)/shard_map/convert_element_type | solution.py:40
  302.3 0.0 all-gather.2.cloned.1.call-update
  302.3 0.0 all-reduce.2.cloned.1.call-done
  302.3 5.5 %multiply_subtract_fusion = (f32[512,1024]{1,0:T(8,128)}, f32[512,1024]{1,0:T(8,128)}) fusion(f32[512,1024]{1,0:T(8,128)S(1)} %copy-done.2, f32[512,1024]{1,0:T(8,128)} %all-reduce.2.cloned.1.call-done, f32[512,1024]{1,0:T(8,128)} %param.15), kind=kLoop, calls=%fused_computation.12 | loop fusion | flops 3670016 | bytes 10485760 | tf_op jit(solution)/shard_map/sub | solution.py:17
  307.8 106.6 %all-gather.2.cloned.1.call-done = bf16[8192,1024]{1,0:T(8,128)(2,1)} async-done(((bf16[512,1024]{1,0:T(8,128)(2,1)}), bf16[8192,1024]{1,0:T(8,128)(2,1)}) %all-gather.2.cloned.1.call-update) | async-done | bytes 16777232 | tf_op jit(solution)/shard_map/all_gather | solution.py:44
  414.4 0.0 copy-start.1
  414.4 16.0 %fusion.7 = f32[1,512,1024]{1,2,0:T(8,128)} fusion(bf16[8192,1024]{1,0:T(8,128)(2,1)} %all-gather.2.cloned.1.call-done, bf16[1,512,8192]{2,1,0:T(8,128)(2,1)} %param.8), kind=kOutput, calls=%fused_computation.14 | convolution fusion | flops 8589934592 | bytes 27262976 | tf_op jit(solution)/shard_map/dot_general | solution.py:42
  430.4 2.9 copy.14
  433.3 0.0 copy-done.1
Async XLA Ops:
  8.0 1.2 copy-start
  8.0 285.9 %reduce-scatter.2.cloned.1.call-start = ((), (), s32[]{:S(2)}) async-start(), calls=%async_computation.1 | async-start | bytes 35651584 | tf_op jit(solution)/shard_map/reduce_scatter | solution.py:28
  28.0 1.6 copy-start.2
  28.0 274.3 %all-reduce.2.cloned.1.call-start = ((), (), s32[]{:S(2)}) async-start(), calls=%async_computation.3 | async-start | bytes 4194304 | tf_op jit(solution)/shard_map/psum | solution.py:49
  33.0 381.4 %all-gather.2.cloned.1.call-start = ((), (), s32[]{:S(2)}) async-start(), calls=%async_computation.2 | async-start | bytes 17825792 | tf_op jit(solution)/shard_map/all_gather | solution.py:44
  414.4 18.9 %copy-start.1 = (bf16[1,512,1024]{2,1,0:T(8,128)(2,1)S(1)}, bf16[1,512,1024]{2,1,0:T(8,128)(2,1)}, u32[]{:S(2)}) copy-start(bf16[1,512,1024]{2,1,0:T(8,128)(2,1)} %param.9) | copy-start | bytes 3145732
Sparse Core Ops, SparseCore 0:
  28.1 265.8 reduce-scatter.1
  302.4 111.9 all-gather.1
Sparse Core Ops, SparseCore 1:
  33.1 140.4 all-reduce.1
where the time goes:
time: 441 us
  waiting for transfers between devices  367 us (83%)
  matrix products  34.7 us (8%)
  other arithmetic  17.2 us (4%)
  between operations  15.5 us (4%)
  local copies, waits for them, and re-layouts  5.58 us (1%)
    reduce_scatter x1, waiting for transfers between devices, per_device(): lax.psum_scatter(lax.dot_general(feature_slab, upstream, (((0,), (0,)), (...  261 us
    all_gather x1, waiting for transfers between devices, per_device(): lax.all_gather(weight_bf, 'fsdp', axis=0, tiled=True)  107 us
    dot_general x1, matrix products, per_device(): lax.dot_general(feature_slab, upstream, (((0,), (0,)), ((), ())), preferr...  18.7 us
    dot_general x1, matrix products, per_device(): jnp.dot(feature_slab, lax.all_gather(weight_bf, 'fsdp', axis=0, tiled=Tru...  16 us
  transfers between devices with their start and end apart: 3, of which 2 were waited for; matrix products, arithmetic and copies ran while one was open for 4% of the time, Pallas kernels for 0%

commit v1 on v0

v1 whole, which is shorter than its diff:
```python
import functools

import jax
import jax.numpy as jnp
from jax import lax
from jax.experimental import pallas as pl
from jax.experimental.pallas import tpu as pltpu
from jax.sharding import PartitionSpec as P

BETA_ONE = 0.9
BETA_TWO = 0.95
INNER_RATE = 0.002
DECAY_RATE = 0.1
EPSILON = 1e-08
OUTER_RATE = 0.7
OUTER_MOMENT = 0.9

BF = jnp.bfloat16
F32 = jnp.float32

N_Y = 4
N_FSDP = 16
N_ISLAND = 8
CHEAP = pl.CostEstimate(flops=1, bytes_accessed=1, transcendentals=0)


def place(x_hi, y, core):
    return (x_hi % 2) * 8 + (y % N_Y) * 2 + core % 2


def moves(d_x, d_y, d_core):
    pairs = []
    for index in range(N_FSDP):
        x_hi, y, core = index // 8, (index // 2) % N_Y, index % 2
        pairs.append((index, place(x_hi + d_x, y + d_y, core + d_core)))
    return pairs


SPLIT = 640

SWAP = moves(0, 0, 1)
ACROSS = moves(1, 0, 0)
UP = moves(0, 1, 0)
DOWN = moves(0, -1, 0)


Z_GROUPS = [[2 * z + x_lo for z in range(4)] for x_lo in range(2)]
X_LO = [(i, i ^ 1) for i in range(N_ISLAND)]


def send(value, pairs):
    return lax.ppermute(value, "fsdp", pairs)


class Line:
    def __init__(self):
        self.mark = ()

    def step(self, *values):
        out = lax.optimization_barrier((*values, *self.mark))[: len(values)]
        self.mark = tuple(out)
        return out[0] if len(values) == 1 else out

    def hold(self, *values):
        out = lax.optimization_barrier((*values, *self.mark))[: len(values)]
        return out[0] if len(values) == 1 else out


def shape(dims, dtype):
    return jax.ShapeDtypeStruct(dims, dtype)


def kernel_call(body, where, operands, grid, in_specs, out_specs, out_shape, scratch=(), alias=None, room=20):
    return pl.pallas_call(
        body,
        out_shape=out_shape,
        grid_spec=pltpu.PrefetchScalarGridSpec(
            num_scalar_prefetch=1,
            grid=grid,
            in_specs=in_specs,
            out_specs=out_specs,
            scratch_shapes=list(scratch),
        ),
        input_output_aliases=alias or {},
        compiler_params=pltpu.CompilerParams(vmem_limit_bytes=room * 1024 * 1024),
        cost_estimate=CHEAP,
    )(where, *operands)


def split_body(where, theirs, mine, sent, kept):
    sent[...] = theirs[...]
    kept[...] = mine[...]


def split_columns(tokens, where, rows):
    count = tokens.shape[0]
    steps = where.shape[0] // 2
    block = pl.BlockSpec((count, rows), lambda i, where: (0, i))
    return kernel_call(
        split_body,
        where,
        (tokens, tokens),
        (steps,),
        [
            pl.BlockSpec((count, rows), lambda i, where: (0, where[i])),
            pl.BlockSpec((count, rows), lambda i, where: (0, where[steps + i])),
        ],
        [block, block],
        [
            shape((count, steps * rows), tokens.dtype),
            shape((2 * count, steps * rows), tokens.dtype),
        ],
        room=8,
    )


def fill_body(where, source, old, out):
    out[...] = source[...]


def fill_lower(source, old):
    count, width = source.shape
    size = width // 3
    return kernel_call(
        fill_body,
        jnp.zeros((1,), jnp.int32),
        (source, old),
        (3,),
        [
            pl.BlockSpec((count, size), lambda i, where: (0, i)),
            pl.BlockSpec(memory_space=pl.ANY),
        ],
        pl.BlockSpec((count, size), lambda i, where: (1, i)),
        shape(old.shape, old.dtype),
        alias={2: 0},
        room=8,
    )


def keys_body(joined, where, *refs):
    number = len(joined)
    lhs, refs, out = refs[:number], list(refs[number:-1]), refs[-1]
    weights = []
    for whole in joined:
        first = refs.pop(0)
        weights.append((first, first) if whole else (first, refs.pop(0)))
    for k, part in enumerate((slice(0, SPLIT), slice(SPLIT, None))):
        total = refs[0][:, part] if refs else None
        for features, pair, whole in zip(lhs, weights, joined):
            weight = pair[k][:, part] if whole else pair[k][...]
            value = jnp.dot(features[...], weight, preferred_element_type=F32)
            total = value if total is None else total + value
        out[:, part] = total


def keys_call(rows, first, count, terms, before=None):
    tile = min(256, count)
    skip = first // tile
    size = key_width(terms[0][1])
    operands, specs = [], []
    for (array, at), _ in terms:
        operands.append(array)
        specs.append(pl.BlockSpec((tile, rows), functools.partial(lambda at, i, where: (i + skip, at), at)))
    for _, parts in terms:
        for part in parts:
            operands.append(part)
            specs.append(pl.BlockSpec(part.shape, lambda i, where: (0, 0)))
    if before is not None:
        operands.append(before)
        specs.append(pl.BlockSpec((tile, size), lambda i, where: (i + skip, 0)))
    return kernel_call(
        functools.partial(keys_body, [len(parts) == 1 for _, parts in terms]),
        jnp.zeros((1,), jnp.int32),
        operands,
        (count // tile,),
        specs,
        pl.BlockSpec((tile, size), lambda i, where: (i, 0)),
        shape((count, size), F32),
    )


def key_width(parts):
    return sum(part.shape[1] for part in parts)


def pieces_body(where, near_up, near_dn, across, other, near, low, high):
    count, half = near_up.shape[0], near_up.shape[0] // 2
    other[...] = across[:, :SPLIT]
    near[:count] = near_up[:, SPLIT:]
    near[count:] = near_dn[:, SPLIT:]
    low[...] = near_dn[:half]
    high[...] = near_up[half:]


def gather_pieces(near_up, near_dn, across):
    rows, width = across.shape
    outs = [
        (rows, SPLIT),
        (2 * rows, width - SPLIT),
        (rows // 2, width),
        (rows // 2, width),
    ]
    full = lambda dims: pl.BlockSpec(dims, lambda i, where: (0, 0))
    return kernel_call(
        pieces_body,
        jnp.zeros((1,), jnp.int32),
        (near_up, near_dn, across),
        (1,),
        [full((rows, width))] * 3,
        [full(dims) for dims in outs],
        [shape(dims, across.dtype) for dims in outs],
        room=16,
    )


def wide(value):
    return value.astype(F32)


def per_device(
    tokens, key_grad_out, key_master, key_first, key_second, frag_local, frag_anchor, frag_momentum
):
    me = lax.axis_index("fsdp")
    x_hi, y, core = me // 8, (me // 2) % N_Y, me % 2
    tok = tokens[0]
    up = key_grad_out[0]
    count, width = tok.shape
    rows = width // N_FSDP
    half = rows // 2
    line = Line()

    def spots(which_core, *blocks):
        return jnp.stack([place(x_hi + p, y + r, which_core) for r, p in blocks]).astype(jnp.int32)

    def far_columns(source, which_core):
        return jnp.concatenate(
            [
                lax.dynamic_slice(
                    source, (0, place(x_hi + p, y + 2, which_core) * rows), (count, rows)
                )
                for p in range(2)
            ],
            axis=1,
        )

    rest_blocks = ((1, 0), (1, 1), (0, 1), (3, 1), (3, 0), (0, 0))

    other_up = send(up, SWAP)
    far_sent = line.step(far_columns(tok, 1 - core))
    got_far = send(far_sent, SWAP)
    share = lax.psum_scatter(
        line.step(frag_anchor - frag_local[0]),
        "island",
        scatter_dimension=0,
        axis_index_groups=Z_GROUPS,
        tiled=True,
    )
    other_up, got_far = line.step(other_up, got_far)
    up_all = jnp.concatenate([up, other_up], axis=0)
    far_all = jnp.concatenate([far_columns(tok, core), got_far], axis=0)
    up_a, up_b = up_all[:, :SPLIT], up_all[:, SPLIT:]

    def transposed(lhs, upstream):
        return lax.dot_general(
            lhs, upstream, (((0,), (0,)), ((), ())), preferred_element_type=F32
        )

    def rest_term(first, number, upstream):
        return transposed(rest_all[:, first * rows : (first + number) * rows], upstream)

    a_far1, a_far0, b_far = line.step(
        transposed(far_all[:, rows:], up_a).astype(BF),
        transposed(far_all[:, :rows], up_a).astype(BF),
        transposed(far_all[:, rows:], up_b).astype(BF),
    )
    a_far1 = send(a_far1, DOWN)
    a_far0 = send(a_far0, UP)
    b_far = send(b_far, ACROSS)

    where = jnp.concatenate([spots(1 - core, *rest_blocks), spots(core, *rest_blocks)])
    rest_sent, rest_kept = line.step(*split_columns(line.hold(tok), where, rows))
    got_rest = send(rest_sent, SWAP)
    got_rest = line.step(got_rest)
    rest_all = line.step(fill_lower(got_rest, rest_kept))
    b_rest = line.step(rest_term(1, 3, up_b).astype(BF))
    b_rest = send(b_rest, ACROSS)
    a_one, a_three = line.step(rest_term(0, 2, up_a), rest_term(3, 2, up_a))
    b_two = line.step(transposed(far_all[:, :rows], up_b))
    share = line.step(share)
    share_other = lax.ppermute(share, "island", X_LO)

    a_far0, a_far1, b_far = line.step(a_far0, a_far1, b_far)
    up_sent = jnp.concatenate([a_one[:rows] + wide(a_far0), a_one[rows:]]).astype(BF)
    down_sent = jnp.concatenate([a_three[:rows] + wide(a_far1), a_three[rows:]]).astype(BF)
    b_low, b_high = (
        (b_two[:half] + wide(b_far[:half])).astype(BF),
        (b_two[half:] + wide(b_far[half:])).astype(BF),
    )
    up_sent, down_sent, b_low, b_high = line.step(up_sent, down_sent, b_low, b_high)
    from_down, from_up = send(up_sent, UP), send(down_sent, DOWN)
    b_low, b_high = send(b_low, UP), send(b_high, DOWN)

    from_down, from_up, rest_all, share_other = line.step(from_down, from_up, rest_all, share_other)
    a_side = rest_term(2, 1, up_a) + wide(from_down[rows:]) + wide(from_up[:rows])
    a_side = line.step(a_side.astype(BF))
    a_side = send(a_side, ACROSS)
    share, rest_all = line.step(share + share_other, rest_all)
    total = lax.all_gather(share, "island", axis=0, axis_index_groups=Z_GROUPS, tiled=True)
    from_down, from_up = line.hold(from_down, from_up)
    a_here = rest_term(5, 1, up_a) + wide(from_down[:rows]) + wide(from_up[rows:])
    a_here = line.step(a_here)
    b_one, b_three = line.step(rest_term(0, 1, up_b), rest_term(4, 2, up_b))

    b_rest, b_low, b_high = line.step(b_rest, b_low, b_high)
    b_up = b_one + wide(b_rest[:rows])
    b_here = b_three[rows:] + wide(b_rest[rows : 2 * rows])
    b_down = b_three[:rows] + wide(b_rest[2 * rows :])
    b_up = jnp.concatenate([b_up[:half] + wide(b_low), b_up[half:]]).astype(BF)
    b_down = jnp.concatenate([b_down[:half], b_down[half:] + wide(b_high)]).astype(BF)
    b_up, b_down, b_here = line.step(b_up, b_down, b_here)
    b_up, b_down = send(b_up, UP), send(b_down, DOWN)

    def inner_update(grad, part):
        master = key_master[0][:, part]
        first_new = BETA_ONE * key_first[0][:, part] + (1.0 - BETA_ONE) * grad
        second_new = BETA_TWO * key_second[0][:, part] + (1.0 - BETA_TWO) * grad * grad
        update = first_new / (jnp.sqrt(second_new) + EPSILON)
        master_new = master - INNER_RATE * (update + DECAY_RATE * master)
        return master_new, first_new, second_new

    a_side, b_up, b_down = line.step(a_side, b_up, b_down)
    grad = jnp.concatenate(
        [a_here + wide(a_side), b_here + wide(b_up) + wide(b_down)], axis=1
    )
    w, grad = line.step(inner_update(grad, slice(None))[0].astype(BF), grad)
    w_dn, w_up, w_x = send(w, UP), send(w, DOWN), send(w, ACROSS)
    states = line.step(*inner_update(grad, slice(None)))
    total, momentum_rows = line.step(total, frag_momentum)
    outer_grad = total / N_ISLAND
    new_momentum = OUTER_MOMENT * momentum_rows + outer_grad
    new_anchor = frag_anchor - OUTER_RATE * (outer_grad + OUTER_MOMENT * new_momentum)
    new_anchor, new_momentum = line.step(new_anchor, new_momentum)

    w_dn, w_up, w_x = line.step(w_dn, w_up, w_x)
    other, near, low, high = line.step(*gather_pieces(w_up, w_dn, w_x))
    near_x = send(near, ACROSS)
    low, high = send(low, UP), send(high, DOWN)
    o_dn, o_up = send(other, UP), send(other, DOWN)
    at = rest_blocks.index
    rest_late = line.hold(rest_all)
    keys = line.step(
        keys_call(
            rows,
            0,
            2 * count,
            [
                ((rest_late, at(b)), (v,))
                for b, v in (((1, 0), w_up), ((3, 0), w_dn), ((0, 0), w), ((0, 1), w_x))
            ],
        )
    )

    near_x, low, high, o_dn, o_up = line.step(near_x, low, high, o_dn, o_up)
    far_low, far_high = low, high
    far_b = jnp.concatenate([low[:, SPLIT:], high[:, SPLIT:]])
    far_b, low, high = line.step(far_b, o_dn[:half], o_up[half:])
    far_x = send(far_b, ACROSS)
    low, high = send(low, UP), send(high, DOWN)
    rest_late, far_low, far_high = line.hold(rest_all, far_low, far_high)
    w_far = jnp.concatenate([far_low, far_high])
    keys = line.step(
        keys_call(
            rows,
            0,
            2 * count,
            [
                ((rest_late, at((1, 1))), (o_up, near_x[:rows])),
                ((rest_late, at((3, 1))), (o_dn, near_x[rows:])),
                ((far_all, 0), (w_far,)),
            ],
            keys,
        )
    )
    far_x, low, high = line.step(far_x, low, high)
    last = [((far_all, 1), (jnp.concatenate([low, high]), far_x))]
    part = line.step(keys_call(rows, count, count, last, keys))
    part = send(part, SWAP)
    mine = keys_call(rows, 0, count, last, keys)
    return (*(v[None] for v in states), (mine + part)[None], new_anchor, new_momentum)


def solution(mesh):
    whole = P("island", "fsdp", None)
    flat = P("fsdp", None)
    return jax.shard_map(
        per_device,
        mesh=mesh,
        in_specs=(whole,) * 6 + (flat, flat),
        out_specs=(whole,) * 4 + (flat, flat),
        check_vma=False,
    )
```

time: 441 us -> 217 us (0.49)
  waiting for transfers between devices: 367 us -> 52 us
  starting transfers between devices: 0.3 us -> 42.7 us
  Pallas kernels: 0 us -> 24 us
  other arithmetic: 17.2 us -> 33.9 us
  local copies, waits for them, and re-layouts: 5.58 us -> 16.8 us
    reduce_scatter x1, waiting for transfers between devices: 261 us -> 0.77 us  [per_device(): lax.psum_scatter(line.step(frag_anchor - frag_local[0]), 'island', scatte...]
    all_gather x1, waiting for transfers between devices: 107 us -> 0.01 us  [per_device(): lax.all_gather(share, 'island', axis=0, axis_index_groups=Z_GROUPS, tiled...]
    ppermute x0 -> x27, waiting for transfers between devices: none -> 51.2 us  [the longest x26 42.6 us: send(): return lax.ppermute(value, 'fsdp', pairs)]
    ppermute x0 -> x27, starting transfers between devices: none -> 42.6 us  [the longest x26 41.4 us: send(): return lax.ppermute(value, 'fsdp', pairs)]
    pallas_call x0 -> x7, Pallas kernels: none -> 24 us  [kernel_call(): pl.pallas_call(body, out_shape=out_shape, grid_spec=pltpu.PrefetchScalarG...]
    add x0 -> x5, other arithmetic: none -> 9.95 us  [the longest x1 6.09 us: per_device(): new_momentum = OUTER_MOMENT * momentum_rows + outer_grad]
    unnamed x7 -> x49, local copies, waits for them, and re-layouts: 5.58 us -> 13.6 us
    concatenate x0 -> x10, other arithmetic: none -> 7.3 us  [the longest x1 2.5 us: per_device(): jnp.concatenate([a_here + wide(a_side), b_here + wide(b_up) + wide(b_down...]
  transfers between devices with their start and end apart: 3 -> 29, of which waited for: 2 -> 9; matrix products, arithmetic and copies ran while one was open for 4% -> 23% of each run, Pallas kernels for 0% -> 8%
where the time goes in v1:
time: 217 us; the launch traced here: 216 us
  waiting for transfers between devices  52 us (24%)
  starting transfers between devices  42.7 us (20%)
  other arithmetic  33.9 us (16%)
  matrix products  32.3 us (15%)
  Pallas kernels  24 us (11%)
  local copies, waits for them, and re-layouts  16.8 us (8%)
  between operations  14.7 us (7%)
    ppermute x26, waiting for transfers between devices, send(): return lax.ppermute(value, 'fsdp', pairs)  42.6 us
    ppermute x26, starting transfers between devices, send(): return lax.ppermute(value, 'fsdp', pairs)  41.4 us
    dot_general x11, matrix products, transposed(): lax.dot_general(lhs, upstream, (((0,), (0,)), ((), ())), preferred_elemen...  32.3 us
    pallas_call x7, Pallas kernels, kernel_call(): pl.pallas_call(body, out_shape=out_shape, grid_spec=pltpu.PrefetchScalarG...  24 us
    unnamed x49, local copies, waits for them, and re-layouts  13.6 us
    ppermute x1, waiting for transfers between devices, per_device(): share_other = lax.ppermute(share, 'island', X_LO)  8.65 us
    add x1, other arithmetic, per_device(): new_momentum = OUTER_MOMENT * momentum_rows + outer_grad  6.09 us
    another operation x3, other arithmetic  4.34 us
  transfers between devices with their start and end apart: 29, of which 9 were waited for; matrix products, arithmetic and copies ran while one was open for 23% of the time, Pallas kernels for 8%

profile of v1, /device:TPU:1, one launch (start us, length us, event | category | flops | bytes accessed | tf_op | source)
XLA Modules:
  0.0 216.3 jit_solution(17678301447683228161)
XLA Ops:
  7.4 2.7 %dynamic-slice_bitcast_fusion.1 = (bf16[512,512]{1,0:T(8,128)(2,1)}, bf16[512,512]{1,0:T(8,128)(2,1)S(1)}, bf16[512,512]{1,0:T(8,128)(2,1)S(1)}, bf16[512,512]{1,0:T(8,128)(2,1)}) fusion(bf16[1,512,8192]{2,1,0:T(8,128)(2,1)} %param.8, s32[]{:T(128)S(6)} %select_n.153, s32[]{:T(128)S(6)} %select_n.151, s32[]{:T(128)S(6)} %select_n.149, s32[]{:T(128)S(6)} %select_n.154), kind=kLoop, calls=%fused_computation.65 | loop fusion | bytes 4194320 | tf_op jit(solution)/shard_map/dynamic_slice | solution.py:238
  12.6 3.3 %bitcast_subtract_fusion = f32[512,1024]{1,0:T(8,128)} fusion(f32[512,1024]{1,0:T(8,128)S(1)} %copy-done.4, f32[1,512,1024]{2,1,0:T(8,128)} %param.13), kind=kLoop, calls=%fused_computation.15 | loop fusion | flops 524288 | bytes 6291456 | tf_op jit(solution)/shard_map/sub | solution.py:252
  17.8 1.5 pad_maximum_fusion.2
  19.5 1.8 pad_maximum_fusion.refs_2_.refs_0_
  21.2 1.9 convolution_convert_fusion
  23.1 1.9 convolution_convert_fusion.1
  25.0 1.5 convolution_convert_fusion.2
  26.5 3.8 %shard_map.127 = (bf16[512,3072]{1,0:T(8,128)(2,1)}, bf16[1024,3072]{1,0:T(8,128)(2,1)S(1)}) custom-call(s32[12]{0:T(128)S(1)} %concatenate.47.where, bf16[512,8192]{1,0:T(8,128)(2,1)S(1)} %bitcast.70, bf16[512,8192]{1,0:T(8,128)(2,1)S(1)} %bitcast.71), custom_call_target="tpu_custom_call" | custom-call | flops 1 | bytes 1 | tf_op jit(solution)/shard_map/pallas_call | solution.py:74
  30.4 2.6 %copy-done = bf16[1024,3072]{1,0:T(8,128)(2,1)} copy-done((bf16[1024,3072]{1,0:T(8,128)(2,1)}, bf16[1024,3072]{1,0:T(8,128)(2,1)S(1)}, u32[]{:S(2)}) %copy-start) | copy-done | bytes 6291480
  34.9 1.5 collective-permute-start.4
  36.4 2.7 %collective-permute-start.5 = (bf16[512,384]{1,0:T(8,128)(2,1)}, bf16[512,384]{1,0:T(8,128)(2,1)}, u32[]{:S(2)}, u32[]{:S(2)}) collective-permute-start(bf16[512,384]{1,0:T(8,128)(2,1)} %convolution_convert_fusion.2), channel_id=1, source_target_pairs={{0,8},{1,9},{2,10},{3,11},{4,12},{5,13},{6,14},{7,15},{8,0},{9,1},... | collective-permute-start | bytes 1179656 | tf_op jit(solution)/shard_map/ppermute | solution.py:52
  39.2 2.8 %fusion.32 = f32[512,384]{1,0:T(8,128)} fusion(bf16[1024,384]{1,0:T(8,128)(2,1)} %copy-done.16, bf16[1024,1024]{1,0:T(8,128)(2,1)S(1)} %pad_maximum_fusion.refs_2_.refs_0_), kind=kOutput, calls=%fused_computation.57 | convolution fusion | flops 402653184 | bytes 2621440 | tf_op jit(solution)/shard_map/dot_general | solution.py:264
  41.9 2.9 %copy-done.1 = bf16[1024,3072]{1,0:T(8,128)(2,1)S(1)} copy-done((bf16[1024,3072]{1,0:T(8,128)(2,1)S(1)}, bf16[1024,3072]{1,0:T(8,128)(2,1)}, u32[]{:S(2)}) %copy-start.1) | copy-done | bytes 6291480
  44.9 2.9 %shard_map.128.refs_0_.refs_1_.refs_2_.refs_3_ = bf16[1024,3072]{1,0:T(8,128)(2,1)S(1)} custom-call(s32[1]{0:T(128)} %constant.183.clone.1.where, bf16[512,3072]{1,0:T(8,128)(2,1)} %collective-permute-done.2.source, bf16[1024,3072]{1,0:T(8,128)(2,1)S(1)} %copy-done.1), custom_call_target="tpu_custom_call", output_to_operand_aliasing={{}: (2, {})} | custom-call | flops 1 | bytes 1 | tf_op jit(solution)/shard_map/pallas_call | solution.py:74
  47.8 2.6 %copy-done.2 = bf16[1024,3072]{1,0:T(8,128)(2,1)} copy-done((bf16[1024,3072]{1,0:T(8,128)(2,1)}, bf16[1024,3072]{1,0:T(8,128)(2,1)S(1)}, u32[]{:S(2)}) %copy-start.2) | copy-done | bytes 6291480
  50.4 4.8 %fusion.2 = bf16[1536,384]{1,0:T(8,128)(2,1)} fusion(bf16[1024,384]{1,0:T(8,128)(2,1)S(1)} %copy-done.17, bf16[1024,3072]{1,0:T(8,128)(2,1)} %copy-done.2), kind=kOutput, calls=%fused_computation.4 | convolution fusion | flops 1208549376 | bytes 5111808 | tf_op jit(solution)/shard_map/dot_general | solution.py:264
  55.2 3.5 %fusion.17 = f32[1024,640]{1,0:T(8,128)S(1)} fusion(bf16[1024,640]{1,0:T(8,128)(2,1)S(1)} %pad_maximum_fusion.2, bf16[1024,3072]{1,0:T(8,128)(2,1)} %copy-done.2), kind=kOutput, calls=%fused_computation.27 | convolution fusion | flops 1342177280 | bytes 6029312 | tf_op jit(solution)/shard_map/dot_general | solution.py:264
  58.7 4.4 %fusion.19 = f32[1024,640]{1,0:T(8,128)S(1)} fusion(bf16[1024,640]{1,0:T(8,128)(2,1)S(1)} %pad_maximum_fusion.2, bf16[1024,3072]{1,0:T(8,128)(2,1)} %copy-done.2), kind=kOutput, calls=%fused_computation.29 | convolution fusion | flops 1342177280 | bytes 6029312 | tf_op jit(solution)/shard_map/dot_general | solution.py:264
  65.5 2.1 add_convert_fusion.2
  67.6 2.4 %add_convert_fusion = (bf16[512,640]{1,0:T(8,128)(2,1)S(1)}, bf16[512,640]{1,0:T(8,128)(2,1)S(1)}) fusion(bf16[512,640]{1,0:T(8,128)(2,1)} %collective-permute-done.4, f32[1024,640]{1,0:T(8,128)} %copy-done.11, bf16[512,640]{1,0:T(8,128)(2,1)} %collective-permute-done.3, f32[1024,640]{1,0:T(8,128)} %copy-done.12), kind=kLoop, calls=%fused_computation.45 | loop fusion | flops 1966080 | bytes 5242880 | tf_op jit(solution)/shard_map/convert.6
  74.1 2.4 %collective-permute-start.10 = (bf16[1536,384]{1,0:T(8,128)(2,1)}, bf16[1536,384]{1,0:T(8,128)(2,1)}, u32[]{:S(2)}, u32[]{:S(2)}) collective-permute-start(bf16[1536,384]{1,0:T(8,128)(2,1)} %fusion.2), channel_id=1, source_target_pairs={{0,8},{1,9},{2,10},{3,11},{4,12},{5,13},{6,14},{7,15},{8,0},{9,1},... | collective-permute-start | bytes 3538952 | tf_op jit(solution)/shard_map/ppermute | solution.py:52
  76.5 8.6 %collective-permute-done.8 = f32[128,1024]{1,0:T(8,128)S(1)} collective-permute-done((f32[128,1024]{1,0:T(8,128)S(1)}, f32[128,1024]{1,0:T(8,128)S(1)}, u32[]{:S(2)}, u32[]{:S(2)}) %collective-permute-start.8) | collective-permute-done | bytes 524320 | tf_op jit(solution)/shard_map/ppermute | solution.py:290
  86.4 14.9 %collective-permute-done.6 = bf16[1024,640]{1,0:T(8,128)(2,1)S(1)} collective-permute-done((bf16[1024,640]{1,0:T(8,128)(2,1)S(1)}, bf16[1024,640]{1,0:T(8,128)(2,1)S(1)}, u32[]{:S(2)}, u32[]{:S(2)}) %collective-permute-start.6) | collective-permute-done | bytes 1310752 | tf_op jit(solution)/shard_map/ppermute | solution.py:52
  101.3 3.9 %fusion.24 = bf16[512,640]{1,0:T(8,128)(2,1)} fusion(bf16[1024,640]{1,0:T(8,128)(2,1)S(1)} %copy-done.14, bf16[1024,3072]{1,0:T(8,128)(2,1)} %copy-done.2, bf16[1024,640]{1,0:T(8,128)(2,1)S(1)} %collective-permute-done.7, bf16[1024,640]{1,0:T(8,128)(2,1)S(1)} %collective-permute-done.6), kind=kOutput, calls=%fused_computation.36 | convolution fusion | flops 672727040 | bytes 4325376 | tf_op jit(solution)/shard_map/dot_general | solution.py:264
  106.1 2.6 %collective-permute-start.9 = (bf16[512,640]{1,0:T(8,128)(2,1)}, bf16[512,640]{1,0:T(8,128)(2,1)}, u32[]{:S(2)}, u32[]{:S(2)}) collective-permute-start(bf16[512,640]{1,0:T(8,128)(2,1)} %fusion.24), channel_id=1, source_target_pairs={{0,8},{1,9},{2,10},{3,11},{4,12},{5,13},{6,14},{7,15},{8,0},{9,1},... | collective-permute-start | bytes 1966088 | tf_op jit(solution)/shard_map/ppermute | solution.py:52
  108.8 2.7 %fusion.22 = f32[512,640]{1,0:T(8,128)S(1)} fusion(bf16[1024,640]{1,0:T(8,128)(2,1)S(1)} %copy-done.15, bf16[1024,3072]{1,0:T(8,128)(2,1)} %copy-done.2, bf16[1024,640]{1,0:T(8,128)(2,1)} %copy-done.21, bf16[1024,640]{1,0:T(8,128)(2,1)} %copy-done.20), kind=kOutput, calls=%fused_computation.33 | convolution fusion | flops 672399360 | bytes 4980736 | tf_op jit(solution)/shard_map/dot_general | solution.py:264
  111.5 2.9 %fusion.15 = f32[1024,384]{1,0:T(8,128)S(1)} fusion(bf16[1024,384]{1,0:T(8,128)(2,1)S(1)} %copy-done.18, bf16[1024,3072]{1,0:T(8,128)(2,1)} %copy-done.2), kind=kOutput, calls=%fused_computation.25 | convolution fusion | flops 805306368 | bytes 4456448 | tf_op jit(solution)/shard_map/dot_general | solution.py:264
  114.4 2.0 fusion.25
  120.7 2.1 collective-permute-start.14
  122.8 6.3 %collective-permute-done.13 = bf16[512,384]{1,0:T(8,128)(2,1)S(1)} collective-permute-done((bf16[512,384]{1,0:T(8,128)(2,1)S(1)}, bf16[512,384]{1,0:T(8,128)(2,1)S(1)}, u32[]{:S(2)}, u32[]{:S(2)}) %collective-permute-start.13) | collective-permute-done | bytes 393248 | tf_op jit(solution)/shard_map/ppermute | solution.py:52
  131.6 2.5 %pad_maximum_fusion.1 = (f32[512,1024]{1,0:T(8,128)S(1)}, bf16[512,1024]{1,0:T(8,128)(2,1)}) fusion(f32[512,384]{1,0:T(8,128)S(1)} %convert_add_fusion.1, f32[512,640]{1,0:T(8,128)S(1)} %convert_add_fusion, f32[1,512,1024]{2,1,0:T(8,128)S(1)} %copy-done.6, f32[1,512,1024]{2,1,0:T(8,128)S(1)} %copy-done.7, f32[1,512,1024]{2,1,0:T(8,128)S(1)} %copy-done.5), kind=kLoop, calls=%fused_computation.14 | loop fusion | flops 7864320 | bytes 11534336 | tf_op jit(solution)/shard_map/concatenate | solution.py:332
  134.1 2.7 %collective-permute-start.16 = (bf16[512,1024]{1,0:T(8,128)(2,1)}, bf16[512,1024]{1,0:T(8,128)(2,1)}, u32[]{:S(2)}, u32[]{:S(2)}) collective-permute-start(bf16[512,1024]{1,0:T(8,128)(2,1)} %get-tuple-element.137.refs_6_), channel_id=1, source_target_pairs={{0,6},{1,7},{2,0},{3,1},{4,2},{5,3},{6,4},{7,5},{8,14},{9,15},{10,... | collective-permute-start | bytes 3145736 | tf_op jit(solution)/shard_map/ppermute | solution.py:52
  137.6 4.1 %bitcast_subtract_fusion.1 = (f32[512,1024]{1,0:T(8,128)}, f32[512,1024]{1,0:T(8,128)}, f32[512,1024]{1,0:T(8,128)}) fusion(f32[1,512,1024]{2,1,0:T(8,128)S(1)} %copy-done.5, f32[512,1024]{1,0:T(8,128)S(1)} %get-tuple-element.136, f32[1,512,1024]{2,1,0:T(8,128)S(1)} %copy-done.6, f32[1,512,1024]{2,1,0:T(8,128)S(1)} %copy-done.7), kind=kLoop, calls=%fused_computation.18 | loop fusion | flops 6815744 | bytes 14680064 | tf_op jit(solution)/shard_map/sub | solution.py:328
  141.7 6.1 %multiply_add_fusion = (f32[512,1024]{1,0:T(8,128)}, f32[512,1024]{1,0:T(8,128)}) fusion(f32[512,1024]{1,0:T(8,128)} %param.15, f32[512,1024]{1,0:T(8,128)} %all-gather.2.cloned.1.call-done, f32[512,1024]{1,0:T(8,128)} %param.14), kind=kLoop, calls=%fused_computation.24 | loop fusion | flops 3670016 | bytes 10485760 | tf_op jit(solution)/shard_map/add | solution.py:340
  147.8 8.6 %collective-permute-done.15.near_dn.refs_5_ = bf16[512,1024]{1,0:T(8,128)(2,1)S(1)} collective-permute-done((bf16[512,1024]{1,0:T(8,128)(2,1)}, bf16[512,1024]{1,0:T(8,128)(2,1)S(1)}, u32[]{:S(2)}, u32[]{:S(2)}) %collective-permute-start.15) | collective-permute-done | bytes 1048608 | tf_op jit(solution)/shard_map/ppermute | solution.py:52
  156.5 2.4 %collective-permute-done.17.across.refs_7_ = bf16[512,1024]{1,0:T(8,128)(2,1)} collective-permute-done((bf16[512,1024]{1,0:T(8,128)(2,1)}, bf16[512,1024]{1,0:T(8,128)(2,1)}, u32[]{:S(2)}, u32[]{:S(2)}) %collective-permute-start.17) | collective-permute-done | bytes 1048608 | tf_op jit(solution)/shard_map/ppermute | solution.py:52
  158.9 1.7 shard_map.129
  161.9 2.7 %collective-permute-start.22 = (bf16[512,640]{1,0:T(8,128)(2,1)S(1)}, bf16[512,640]{1,0:T(8,128)(2,1)S(1)}, u32[]{:S(2)}, u32[]{:S(2)}) collective-permute-start(bf16[512,640]{1,0:T(8,128)(2,1)S(1)} %get-tuple-element.155), channel_id=1, source_target_pairs={{0,6},{1,7},{2,0},{3,1},{4,2},{5,3},{6,4},{7,5},{8,14},{9,15},{10,... | collective-permute-start | bytes 1966088 | tf_op jit(solution)/shard_map/ppermute | solution.py:52
  164.6 2.7 %collective-permute-start.20 = (bf16[256,1024]{1,0:T(8,128)(2,1)S(1)}, bf16[256,1024]{1,0:T(8,128)(2,1)S(1)}, u32[]{:S(2)}, u32[]{:S(2)}) collective-permute-start(bf16[256,1024]{1,0:T(8,128)(2,1)S(1)} %get-tuple-element.154), channel_id=1, source_target_pairs={{0,6},{1,7},{2,0},{3,1},{4,2},{5,3},{6,4},{7,5},{8,14},{9,15},{10,... | collective-permute-start | bytes 1572872 | tf_op jit(solution)/shard_map/ppermute | solution.py:52
  167.2 2.8 %copy-done.3 = bf16[1024,3072]{1,0:T(8,128)(2,1)S(1)} copy-done((bf16[1024,3072]{1,0:T(8,128)(2,1)S(1)}, bf16[1024,3072]{1,0:T(8,128)(2,1)}, u32[]{:S(2)}) %copy-start.3) | copy-done | bytes 6291480
  170.0 8.3 %shard_map.130.refs_8_ = f32[1024,1024]{1,0:T(8,128)S(1)} custom-call(s32[1]{0:T(128)} %constant.183.clone.1.where, bf16[1024,3072]{1,0:T(8,128)(2,1)S(1)} %copy-done.3, bf16[1024,3072]{1,0:T(8,128)(2,1)S(1)} %copy-done.3, bf16[1024,3072]{1,0:T(8,128)(2,1)S(1)} %copy-done.3, bf16[1024,3072]{1,0:T(8,128)(2,1)S(1)} %copy-done.3, ...), custom_call_target="tpu_custom_call" | custom-call | flops 1 | bytes 1 | tf_op jit(solution)/shard_map/pallas_call | solution.py:74
  178.3 7.0 %collective-permute-done.19 = bf16[256,1024]{1,0:T(8,128)(2,1)S(1)} collective-permute-done((bf16[256,1024]{1,0:T(8,128)(2,1)S(1)}, bf16[256,1024]{1,0:T(8,128)(2,1)S(1)}, u32[]{:S(2)}, u32[]{:S(2)}) %collective-permute-start.19) | collective-permute-done | bytes 524320 | tf_op jit(solution)/shard_map/ppermute | solution.py:52
  185.5 1.6 collective-permute-start.23
  187.1 2.7 %collective-permute-start.25 = (bf16[256,640]{1,0:T(8,128)(2,1)S(1)}, bf16[256,640]{1,0:T(8,128)(2,1)S(1)}, u32[]{:S(2)}, u32[]{:S(2)}) collective-permute-start(bf16[256,640]{1,0:T(8,128)(2,1)S(1)} %slice.155), channel_id=1, source_target_pairs={{0,6},{1,7},{2,0},{3,1},{4,2},{5,3},{6,4},{7,5},{8,14},{9,15},{10,... | collective-permute-start | bytes 983048 | tf_op jit(solution)/shard_map/ppermute | solution.py:52
  189.9 5.1 %shard_map.131.refs_3_ = f32[1024,1024]{1,0:T(8,128)S(1)} custom-call(s32[1]{0:T(128)} %constant.183.clone.1.where, bf16[1024,3072]{1,0:T(8,128)(2,1)S(1)} %copy-done.3, bf16[1024,3072]{1,0:T(8,128)(2,1)S(1)} %copy-done.3, bf16[1024,1024]{1,0:T(8,128)(2,1)S(1)} %pad_maximum_fusion.refs_2_.refs_0_, bf16[512,640]{1,0:T(8,128)(2,1)S(1)} %collective-permute-done.22.refs_3_, ...), custom_call_target="tpu_custom_call" | custom-call | flops 1 | bytes 1 | tf_op jit(solution)/shard_map/pallas_call | solution.py:74
  196.2 7.7 %collective-permute-start.26 = (f32[512,1024]{1,0:T(8,128)S(1)}, f32[512,1024]{1,0:T(8,128)S(1)}, u32[]{:S(2)}, u32[]{:S(2)}) collective-permute-start(f32[512,1024]{1,0:T(8,128)S(1)} %shard_map.133), channel_id=1, source_target_pairs={{0,1},{1,0},{2,3},{3,2},{4,5},{5,4},{6,7},{7,6},{8,9},{9,8},{10,11... | collective-permute-start | bytes 6291464 | tf_op jit(solution)/shard_map/ppermute | solution.py:52
  205.0 2.7 %collective-permute-done.26 = f32[512,1024]{1,0:T(8,128)S(1)} collective-permute-done((f32[512,1024]{1,0:T(8,128)S(1)}, f32[512,1024]{1,0:T(8,128)S(1)}, u32[]{:S(2)}, u32[]{:S(2)}) %collective-permute-start.26) | collective-permute-done | bytes 2097184 | tf_op jit(solution)/shard_map/ppermute | solution.py:52
  207.7 1.7 add_bitcast_fusion
  (115 shorter events, 26.5 us)
Async XLA Ops:
  7.2 58.3 %reduce-scatter.2.cloned.1.call-start = ((), (), s32[]{:S(2)}) async-start(), calls=%async_computation.1 | async-start | bytes 2621440 | tf_op jit(solution)/shard_map/reduce_scatter | solution.py:251
  7.4 5.3 %copy-start.8 = (bf16[1,512,1024]{2,1,0:T(8,128)(2,1)S(1)}, bf16[1,512,1024]{2,1,0:T(8,128)(2,1)}, u32[]{:S(2)}) copy-start(bf16[1,512,1024]{2,1,0:T(8,128)(2,1)} %param.9) | copy-start | bytes 3145732
  10.1 2.5 %copy-start.4 = (f32[512,1024]{1,0:T(8,128)S(1)}, f32[512,1024]{1,0:T(8,128)}, u32[]{:S(2)}) copy-start(f32[512,1024]{1,0:T(8,128)} %param.14) | copy-start | bytes 6291460
  11.2 5.5 %collective-permute-start.1 = (bf16[512,1024]{1,0:T(8,128)(2,1)}, bf16[512,1024]{1,0:T(8,128)(2,1)}, u32[]{:S(2)}, u32[]{:S(2)}) collective-permute-start(bf16[512,1024]{1,0:T(8,128)(2,1)} %pad_maximum_fusion.5), channel_id=1, source_target_pairs={{0,1},{1,0},{2,3},{3,2},{4,5},{5,4},{6,7},{7,6},{8,9},{9,8},{10,11... | collective-permute-start | bytes 3145736 | tf_op jit(solution)/shard_map/ppermute | solution.py:52
  12.6 4.1 %collective-permute-start = (bf16[512,1024]{1,0:T(8,128)(2,1)S(1)}, bf16[512,1024]{1,0:T(8,128)(2,1)}, u32[]{:S(2)}, u32[]{:S(2)}) collective-permute-start(bf16[512,1024]{1,0:T(8,128)(2,1)S(1)} %bitcast.72), channel_id=1, source_target_pairs={{0,1},{1,0},{2,3},{3,2},{4,5},{5,4},{6,7},{7,6},{8,9},{9,8},{10,11... | collective-permute-start | bytes 3145736 | tf_op jit(solution)/shard_map/ppermute | solution.py:52
  17.8 7.3 %copy-start.16 = (bf16[1024,384]{1,0:T(8,128)(2,1)}, bf16[1024,384]{1,0:T(8,128)(2,1)S(1)}, u32[]{:S(2)}) copy-start(bf16[1024,384]{1,0:T(8,128)(2,1)S(1)} %pad_maximum_fusion.7) | copy-start | bytes 2359300
  19.3 39.4 %copy-start.13 = (bf16[1024,640]{1,0:T(8,128)(2,1)}, bf16[1024,640]{1,0:T(8,128)(2,1)S(1)}, u32[]{:S(2)}) copy-start(bf16[1024,640]{1,0:T(8,128)(2,1)S(1)} %pad_maximum_fusion.2) | copy-start | bytes 3932164
  21.2 5.3 %slice-start = ((s8[8388608]{0:T(1024)(128)(4,1)}), s8[4194304]{0:T(1024)(128)(4,1)S(1)}, s32[]{:S(2)}) async-start(s8[8388608]{0:T(1024)(128)(4,1)} %bitcast.68), calls=%async_computation.3 | async-start | bytes 8388608
  23.1 3.4 %slice-start.1 = ((s8[8388608]{0:T(1024)(128)(4,1)}), s8[4194304]{0:T(1024)(128)(4,1)S(1)}, s32[]{:S(2)}) async-start(s8[8388608]{0:T(1024)(128)(4,1)} %bitcast.68), calls=%async_computation.4 | async-start | bytes 8388608
  30.4 2.6 %copy-start = (bf16[1024,3072]{1,0:T(8,128)(2,1)}, bf16[1024,3072]{1,0:T(8,128)(2,1)S(1)}, u32[]{:S(2)}) copy-start(bf16[1024,3072]{1,0:T(8,128)(2,1)S(1)} %get-tuple-element.100.old) | copy-start | bytes 18874372
  33.0 8.9 %collective-permute-start.2 = (bf16[512,3072]{1,0:T(8,128)(2,1)}, bf16[512,3072]{1,0:T(8,128)(2,1)}, u32[]{:S(2)}, u32[]{:S(2)}) collective-permute-start(bf16[512,3072]{1,0:T(8,128)(2,1)} %get-tuple-element.99), channel_id=1, source_target_pairs={{0,1},{1,0},{2,3},{3,2},{4,5},{5,4},{6,7},{7,6},{8,9},{9,8},{10,11... | collective-permute-start | bytes 9437192 | tf_op jit(solution)/shard_map/ppermute | solution.py:52
  33.4 108.3 %all-gather.2.cloned.1.call-start = ((), (), s32[]{:S(2)}) async-start(), calls=%async_computation.2 | async-start | bytes 2621440 | tf_op jit(solution)/shard_map/all_gather | solution.py:308
  33.5 32.0 %collective-permute-start.3 = (bf16[512,640]{1,0:T(8,128)(2,1)}, bf16[512,640]{1,0:T(8,128)(2,1)}, u32[]{:S(2)}, u32[]{:S(2)}) collective-permute-start(bf16[512,640]{1,0:T(8,128)(2,1)} %convolution_convert_fusion), channel_id=1, source_target_pairs={{0,2},{1,3},{2,4},{3,5},{4,6},{5,7},{6,0},{7,1},{8,10},{9,11},{10,... | collective-permute-start | bytes 1966088 | tf_op jit(solution)/shard_map/ppermute | solution.py:52
  34.9 30.6 %collective-permute-start.4 = (bf16[512,640]{1,0:T(8,128)(2,1)}, bf16[512,640]{1,0:T(8,128)(2,1)}, u32[]{:S(2)}, u32[]{:S(2)}) collective-permute-start(bf16[512,640]{1,0:T(8,128)(2,1)} %convolution_convert_fusion.1), channel_id=1, source_target_pairs={{0,6},{1,7},{2,0},{3,1},{4,2},{5,3},{6,4},{7,5},{8,14},{9,15},{10,... | collective-permute-start | bytes 1966088 | tf_op jit(solution)/shard_map/ppermute | solution.py:52
  36.4 29.0 %collective-permute-start.5 = (bf16[512,384]{1,0:T(8,128)(2,1)}, bf16[512,384]{1,0:T(8,128)(2,1)}, u32[]{:S(2)}, u32[]{:S(2)}) collective-permute-start(bf16[512,384]{1,0:T(8,128)(2,1)} %convolution_convert_fusion.2), channel_id=1, source_target_pairs={{0,8},{1,9},{2,10},{3,11},{4,12},{5,13},{6,14},{7,15},{8,0},{9,1},... | collective-permute-start | bytes 1179656 | tf_op jit(solution)/shard_map/ppermute | solution.py:52
  41.9 2.9 %copy-start.1 = (bf16[1024,3072]{1,0:T(8,128)(2,1)S(1)}, bf16[1024,3072]{1,0:T(8,128)(2,1)}, u32[]{:S(2)}) copy-start(bf16[1024,3072]{1,0:T(8,128)(2,1)} %copy-done) | copy-start | bytes 18874372
  44.9 5.5 %copy-start.17 = (bf16[1024,384]{1,0:T(8,128)(2,1)S(1)}, bf16[1024,384]{1,0:T(8,128)(2,1)}, u32[]{:S(2)}) copy-start(bf16[1024,384]{1,0:T(8,128)(2,1)} %copy-done.16) | copy-start | bytes 2359300
  47.8 2.6 %copy-start.2 = (bf16[1024,3072]{1,0:T(8,128)(2,1)}, bf16[1024,3072]{1,0:T(8,128)(2,1)S(1)}, u32[]{:S(2)}) copy-start(bf16[1024,3072]{1,0:T(8,128)(2,1)S(1)} %shard_map.128.refs_0_.refs_1_.refs_2_.refs_3_) | copy-start | bytes 18874372
  58.7 4.4 %copy-start.11 = (f32[1024,640]{1,0:T(8,128)}, f32[1024,640]{1,0:T(8,128)S(1)}, u32[]{:S(2)}) copy-start(f32[1024,640]{1,0:T(8,128)S(1)} %fusion.17) | copy-start | bytes 7864324
  69.9 3.0 %copy-start.19 = (f32[128,1024]{1,0:T(8,128)S(1)}, f32[128,1024]{1,0:T(8,128)}, u32[]{:S(2)}) copy-start(f32[128,1024]{1,0:T(8,128)} %reduce-scatter.2.cloned.1.call-done) | copy-start | bytes 1572868
  69.9 31.4 %copy-start.14 = (bf16[1024,640]{1,0:T(8,128)(2,1)S(1)}, bf16[1024,640]{1,0:T(8,128)(2,1)}, u32[]{:S(2)}) copy-start(bf16[1024,640]{1,0:T(8,128)(2,1)} %copy-done.13) | copy-start | bytes 3932164
  70.2 31.1 %collective-permute-start.6 = (bf16[1024,640]{1,0:T(8,128)(2,1)S(1)}, bf16[1024,640]{1,0:T(8,128)(2,1)S(1)}, u32[]{:S(2)}, u32[]{:S(2)}) collective-permute-start(bf16[1024,640]{1,0:T(8,128)(2,1)S(1)} %pad_maximum_fusion.3), channel_id=1, source_target_pairs={{0,2},{1,3},{2,4},{3,5},{4,6},{5,7},{6,0},{7,1},{8,10},{9,11},{10,... | collective-permute-start | bytes 3932168 | tf_op jit(solution)/shard_map/ppermute | solution.py:52
  71.5 29.8 %collective-permute-start.7 = (bf16[1024,640]{1,0:T(8,128)(2,1)S(1)}, bf16[1024,640]{1,0:T(8,128)(2,1)S(1)}, u32[]{:S(2)}, u32[]{:S(2)}) collective-permute-start(bf16[1024,640]{1,0:T(8,128)(2,1)S(1)} %pad_maximum_fusion.4), channel_id=1, source_target_pairs={{0,6},{1,7},{2,0},{3,1},{4,2},{5,3},{6,4},{7,5},{8,14},{9,15},{10,... | collective-permute-start | bytes 3932168 | tf_op jit(solution)/shard_map/ppermute | solution.py:52
  72.9 12.2 %collective-permute-start.8 = (f32[128,1024]{1,0:T(8,128)S(1)}, f32[128,1024]{1,0:T(8,128)S(1)}, u32[]{:S(2)}, u32[]{:S(2)}) collective-permute-start(f32[128,1024]{1,0:T(8,128)S(1)} %copy-done.19), channel_id=1, source_target_pairs={{0,16},{16,0},{32,48},{48,32},{64,80},{80,64},{96,112},{112,96},{1... | collective-permute-start | bytes 1572872 | tf_op jit(solution)/shard_map/ppermute | solution.py:290
  74.1 42.2 %collective-permute-start.10 = (bf16[1536,384]{1,0:T(8,128)(2,1)}, bf16[1536,384]{1,0:T(8,128)(2,1)}, u32[]{:S(2)}, u32[]{:S(2)}) collective-permute-start(bf16[1536,384]{1,0:T(8,128)(2,1)} %fusion.2), channel_id=1, source_target_pairs={{0,8},{1,9},{2,10},{3,11},{4,12},{5,13},{6,14},{7,15},{8,0},{9,1},... | collective-permute-start | bytes 3538952 | tf_op jit(solution)/shard_map/ppermute | solution.py:52
  76.5 39.8 %collective-permute-start.11 = (bf16[256,384]{1,0:T(8,128)(2,1)}, bf16[256,384]{1,0:T(8,128)(2,1)}, u32[]{:S(2)}, u32[]{:S(2)}) collective-permute-start(bf16[256,384]{1,0:T(8,128)(2,1)} %get-tuple-element.113), channel_id=1, source_target_pairs={{0,2},{1,3},{2,4},{3,5},{4,6},{5,7},{6,0},{7,1},{8,10},{9,11},{10,... | collective-permute-start | bytes 589832 | tf_op jit(solution)/shard_map/ppermute | solution.py:52
  85.2 31.2 %collective-permute-start.12 = (bf16[256,384]{1,0:T(8,128)(2,1)}, bf16[256,384]{1,0:T(8,128)(2,1)}, u32[]{:S(2)}, u32[]{:S(2)}) collective-permute-start(bf16[256,384]{1,0:T(8,128)(2,1)} %get-tuple-element.114), channel_id=1, source_target_pairs={{0,6},{1,7},{2,0},{3,1},{4,2},{5,3},{6,4},{7,5},{8,14},{9,15},{10,... | collective-permute-start | bytes 589832 | tf_op jit(solution)/shard_map/ppermute | solution.py:52
  101.3 4.0 %copy-start.20 = (bf16[1024,640]{1,0:T(8,128)(2,1)}, bf16[1024,640]{1,0:T(8,128)(2,1)S(1)}, u32[]{:S(2)}) copy-start(bf16[1024,640]{1,0:T(8,128)(2,1)S(1)} %collective-permute-done.6) | copy-start | bytes 3932164
  101.3 4.0 %copy-start.21 = (bf16[1024,640]{1,0:T(8,128)(2,1)}, bf16[1024,640]{1,0:T(8,128)(2,1)S(1)}, u32[]{:S(2)}) copy-start(bf16[1024,640]{1,0:T(8,128)(2,1)S(1)} %collective-permute-done.7) | copy-start | bytes 3932164
  105.3 3.5 %copy-start.15 = (bf16[1024,640]{1,0:T(8,128)(2,1)S(1)}, bf16[1024,640]{1,0:T(8,128)(2,1)}, u32[]{:S(2)}) copy-start(bf16[1024,640]{1,0:T(8,128)(2,1)} %copy-done.13) | copy-start | bytes 3932164
  106.1 23.0 %collective-permute-start.9 = (bf16[512,640]{1,0:T(8,128)(2,1)}, bf16[512,640]{1,0:T(8,128)(2,1)}, u32[]{:S(2)}, u32[]{:S(2)}) collective-permute-start(bf16[512,640]{1,0:T(8,128)(2,1)} %fusion.24), channel_id=1, source_target_pairs={{0,8},{1,9},{2,10},{3,11},{4,12},{5,13},{6,14},{7,15},{8,0},{9,1},... | collective-permute-start | bytes 1966088 | tf_op jit(solution)/shard_map/ppermute | solution.py:52
  108.7 2.7 %copy-start.18 = (bf16[1024,384]{1,0:T(8,128)(2,1)S(1)}, bf16[1024,384]{1,0:T(8,128)(2,1)}, u32[]{:S(2)}) copy-start(bf16[1024,384]{1,0:T(8,128)(2,1)} %copy-done.16) | copy-start | bytes 2359300
  120.0 10.6 %copy-start.7 = (f32[1,512,1024]{2,1,0:T(8,128)S(1)}, f32[1,512,1024]{2,1,0:T(8,128)}, u32[]{:S(2)}) copy-start(f32[1,512,1024]{2,1,0:T(8,128)} %param.11) | copy-start | bytes 6291460
  120.0 9.0 %collective-permute-start.13 = (bf16[512,384]{1,0:T(8,128)(2,1)S(1)}, bf16[512,384]{1,0:T(8,128)(2,1)S(1)}, u32[]{:S(2)}, u32[]{:S(2)}) collective-permute-start(bf16[512,384]{1,0:T(8,128)(2,1)S(1)} %pad_maximum_fusion.8), channel_id=1, source_target_pairs={{0,2},{1,3},{2,4},{3,5},{4,6},{5,7},{6,0},{7,1},{8,10},{9,11},{10,... | collective-permute-start | bytes 1179656 | tf_op jit(solution)/shard_map/ppermute | solution.py:52
  120.7 8.4 %collective-permute-start.14 = (bf16[512,384]{1,0:T(8,128)(2,1)S(1)}, bf16[512,384]{1,0:T(8,128)(2,1)S(1)}, u32[]{:S(2)}, u32[]{:S(2)}) collective-permute-start(bf16[512,384]{1,0:T(8,128)(2,1)S(1)} %pad_maximum_fusion.9), channel_id=1, source_target_pairs={{0,6},{1,7},{2,0},{3,1},{4,2},{5,3},{6,4},{7,5},{8,14},{9,15},{10,... | collective-permute-start | bytes 1179656 | tf_op jit(solution)/shard_map/ppermute | solution.py:52
  134.1 22.4 %collective-permute-start.15 = (bf16[512,1024]{1,0:T(8,128)(2,1)}, bf16[512,1024]{1,0:T(8,128)(2,1)S(1)}, u32[]{:S(2)}, u32[]{:S(2)}) collective-permute-start(bf16[512,1024]{1,0:T(8,128)(2,1)} %get-tuple-element.137.refs_6_), channel_id=1, source_target_pairs={{0,2},{1,3},{2,4},{3,5},{4,6},{5,7},{6,0},{7,1},{8,10},{9,11},{10,... | collective-permute-start | bytes 3145736 | tf_op jit(solution)/shard_map/ppermute | solution.py:52
  134.1 22.4 %collective-permute-start.16 = (bf16[512,1024]{1,0:T(8,128)(2,1)}, bf16[512,1024]{1,0:T(8,128)(2,1)}, u32[]{:S(2)}, u32[]{:S(2)}) collective-permute-start(bf16[512,1024]{1,0:T(8,128)(2,1)} %get-tuple-element.137.refs_6_), channel_id=1, source_target_pairs={{0,6},{1,7},{2,0},{3,1},{4,2},{5,3},{6,4},{7,5},{8,14},{9,15},{10,... | collective-permute-start | bytes 3145736 | tf_op jit(solution)/shard_map/ppermute | solution.py:52
  136.8 22.1 %collective-permute-start.17 = (bf16[512,1024]{1,0:T(8,128)(2,1)}, bf16[512,1024]{1,0:T(8,128)(2,1)}, u32[]{:S(2)}, u32[]{:S(2)}) collective-permute-start(bf16[512,1024]{1,0:T(8,128)(2,1)} %get-tuple-element.137.refs_6_), channel_id=1, source_target_pairs={{0,8},{1,9},{2,10},{3,11},{4,12},{5,13},{6,14},{7,15},{8,0},{9,1},... | collective-permute-start | bytes 3145736 | tf_op jit(solution)/shard_map/ppermute | solution.py:52
  160.6 24.7 %collective-permute-start.18 = (bf16[1024,384]{1,0:T(8,128)(2,1)S(1)}, bf16[1024,384]{1,0:T(8,128)(2,1)S(1)}, u32[]{:S(2)}, u32[]{:S(2)}) collective-permute-start(bf16[1024,384]{1,0:T(8,128)(2,1)S(1)} %get-tuple-element.152), channel_id=1, source_target_pairs={{0,8},{1,9},{2,10},{3,11},{4,12},{5,13},{6,14},{7,15},{8,0},{9,1},... | collective-permute-start | bytes 2359304 | tf_op jit(solution)/shard_map/ppermute | solution.py:52
  161.9 23.4 %collective-permute-start.21 = (bf16[512,640]{1,0:T(8,128)(2,1)S(1)}, bf16[512,640]{1,0:T(8,128)(2,1)S(1)}, u32[]{:S(2)}, u32[]{:S(2)}) collective-permute-start(bf16[512,640]{1,0:T(8,128)(2,1)S(1)} %get-tuple-element.155), channel_id=1, source_target_pairs={{0,2},{1,3},{2,4},{3,5},{4,6},{5,7},{6,0},{7,1},{8,10},{9,11},{10,... | collective-permute-start | bytes 1966088 | tf_op jit(solution)/shard_map/ppermute | solution.py:52
  161.9 23.4 %collective-permute-start.22 = (bf16[512,640]{1,0:T(8,128)(2,1)S(1)}, bf16[512,640]{1,0:T(8,128)(2,1)S(1)}, u32[]{:S(2)}, u32[]{:S(2)}) collective-permute-start(bf16[512,640]{1,0:T(8,128)(2,1)S(1)} %get-tuple-element.155), channel_id=1, source_target_pairs={{0,6},{1,7},{2,0},{3,1},{4,2},{5,3},{6,4},{7,5},{8,14},{9,15},{10,... | collective-permute-start | bytes 1966088 | tf_op jit(solution)/shard_map/ppermute | solution.py:52
  164.6 20.7 %collective-permute-start.19 = (bf16[256,1024]{1,0:T(8,128)(2,1)S(1)}, bf16[256,1024]{1,0:T(8,128)(2,1)S(1)}, u32[]{:S(2)}, u32[]{:S(2)}) collective-permute-start(bf16[256,1024]{1,0:T(8,128)(2,1)S(1)} %get-tuple-element.153), channel_id=1, source_target_pairs={{0,2},{1,3},{2,4},{3,5},{4,6},{5,7},{6,0},{7,1},{8,10},{9,11},{10,... | collective-permute-start | bytes 1572872 | tf_op jit(solution)/shard_map/ppermute | solution.py:52
  164.6 20.7 %collective-permute-start.20 = (bf16[256,1024]{1,0:T(8,128)(2,1)S(1)}, bf16[256,1024]{1,0:T(8,128)(2,1)S(1)}, u32[]{:S(2)}, u32[]{:S(2)}) collective-permute-start(bf16[256,1024]{1,0:T(8,128)(2,1)S(1)} %get-tuple-element.154), channel_id=1, source_target_pairs={{0,6},{1,7},{2,0},{3,1},{4,2},{5,3},{6,4},{7,5},{8,14},{9,15},{10,... | collective-permute-start | bytes 1572872 | tf_op jit(solution)/shard_map/ppermute | solution.py:52
  167.2 2.8 %copy-start.3 = (bf16[1024,3072]{1,0:T(8,128)(2,1)S(1)}, bf16[1024,3072]{1,0:T(8,128)(2,1)}, u32[]{:S(2)}) copy-start(bf16[1024,3072]{1,0:T(8,128)(2,1)} %copy-done.2) | copy-start | bytes 18874372
  185.5 9.5 %collective-permute-start.23 = (bf16[512,384]{1,0:T(8,128)(2,1)S(1)}, bf16[512,384]{1,0:T(8,128)(2,1)S(1)}, u32[]{:S(2)}, u32[]{:S(2)}) collective-permute-start(bf16[512,384]{1,0:T(8,128)(2,1)S(1)} %pad_maximum_fusion.10), channel_id=1, source_target_pairs={{0,8},{1,9},{2,10},{3,11},{4,12},{5,13},{6,14},{7,15},{8,0},{9,1},... | collective-permute-start | bytes 1179656 | tf_op jit(solution)/shard_map/ppermute | solution.py:52
  187.1 7.9 %collective-permute-start.24 = (bf16[256,640]{1,0:T(8,128)(2,1)S(1)}, bf16[256,640]{1,0:T(8,128)(2,1)S(1)}, u32[]{:S(2)}, u32[]{:S(2)}) collective-permute-start(bf16[256,640]{1,0:T(8,128)(2,1)S(1)} %slice.154), channel_id=1, source_target_pairs={{0,2},{1,3},{2,4},{3,5},{4,6},{5,7},{6,0},{7,1},{8,10},{9,11},{10,... | collective-permute-start | bytes 983048 | tf_op jit(solution)/shard_map/ppermute | solution.py:52
  187.1 7.9 %collective-permute-start.25 = (bf16[256,640]{1,0:T(8,128)(2,1)S(1)}, bf16[256,640]{1,0:T(8,128)(2,1)S(1)}, u32[]{:S(2)}, u32[]{:S(2)}) collective-permute-start(bf16[256,640]{1,0:T(8,128)(2,1)S(1)} %slice.155), channel_id=1, source_target_pairs={{0,6},{1,7},{2,0},{3,1},{4,2},{5,3},{6,4},{7,5},{8,14},{9,15},{10,... | collective-permute-start | bytes 983048 | tf_op jit(solution)/shard_map/ppermute | solution.py:52
  196.2 11.5 %collective-permute-start.26 = (f32[512,1024]{1,0:T(8,128)S(1)}, f32[512,1024]{1,0:T(8,128)S(1)}, u32[]{:S(2)}, u32[]{:S(2)}) collective-permute-start(f32[512,1024]{1,0:T(8,128)S(1)} %shard_map.133), channel_id=1, source_target_pairs={{0,1},{1,0},{2,3},{3,2},{4,5},{5,4},{6,7},{7,6},{8,9},{9,8},{10,11... | collective-permute-start | bytes 6291464 | tf_op jit(solution)/shard_map/ppermute | solution.py:52
  (5 other events, 8.8 us)
Sparse Core Ops, SparseCore 0:
  33.5 31.8 reduce-scatter.1
  108.8 32.5 all-gather.1

commit v2 on v1

--- a/solution.py
+++ b/solution.py
@@ -284,10 +284,11 @@
     rest_all = line.step(fill_lower(got_rest, rest_kept))
     b_rest = line.step(rest_term(1, 3, up_b).astype(BF))
     b_rest = send(b_rest, ACROSS)
-    a_one, a_three = line.step(rest_term(0, 2, up_a), rest_term(3, 2, up_a))
-    b_two = line.step(transposed(far_all[:, :rows], up_b))
+    a_one = line.step(rest_term(0, 2, up_a))
     share = line.step(share)
     share_other = lax.ppermute(share, "island", X_LO)
+    a_three = line.step(rest_term(3, 2, up_a))
+    b_two = line.step(transposed(far_all[:, :rows], up_b))
 
     a_far0, a_far1, b_far = line.step(a_far0, a_far1, b_far)
     up_sent = jnp.concatenate([a_one[:rows] + wide(a_far0), a_one[rows:]]).astype(BF)

time: 217 us -> 201 us (0.926)
  local copies, waits for them, and re-layouts: 16.8 us -> 7.67 us
  waiting for transfers between devices: 52 us -> 59.5 us
  matrix products: 32.3 us -> 26.3 us
  other arithmetic: 33.9 us -> 29.5 us
  Pallas kernels: 24 us -> 20 us
    unnamed x49 -> x41, local copies, waits for them, and re-layouts: 13.6 us -> 5.34 us
    reduce_scatter x1, waiting for transfers between devices: 0.77 us -> 6.9 us  [per_device(): lax.psum_scatter(line.step(frag_anchor - frag_local[0]), 'island', scatte...]
    dot_general x11, matrix products: 32.3 us -> 26.3 us  [transposed(): lax.dot_general(lhs, upstream, (((0,), (0,)), ((), ())), preferred_elemen...]
    pallas_call x7, Pallas kernels: 24 us -> 20 us  [kernel_call(): pl.pallas_call(body, out_shape=out_shape, grid_spec=pltpu.PrefetchScalarG...]
  transfers between devices with their start and end apart: 29 -> 29, of which waited for: 9 -> 9; matrix products, arithmetic and copies ran while one was open for 23% -> 25% of each run, Pallas kernels for 8% -> 9%
where the time goes in v2:
time: 201 us; the launch traced here: 200 us
  waiting for transfers between devices  59.5 us (30%)
  starting transfers between devices  42.7 us (21%)
  other arithmetic  29.5 us (15%)
  matrix products  26.3 us (13%)
  Pallas kernels  20 us (10%)
  between operations  14.8 us (7%)
  local copies, waits for them, and re-layouts  7.67 us (4%)
    ppermute x26, waiting for transfers between devices, send(): return lax.ppermute(value, 'fsdp', pairs)  43.9 us
    ppermute x26, starting transfers between devices, send(): return lax.ppermute(value, 'fsdp', pairs)  41.5 us
    dot_general x11, matrix products, transposed(): lax.dot_general(lhs, upstream, (((0,), (0,)), ((), ())), preferred_elemen...  26.3 us
    pallas_call x7, Pallas kernels, kernel_call(): pl.pallas_call(body, out_shape=out_shape, grid_spec=pltpu.PrefetchScalarG...  20 us
    ppermute x1, waiting for transfers between devices, per_device(): share_other = lax.ppermute(share, 'island', X_LO)  8.63 us
    reduce_scatter x1, waiting for transfers between devices, per_device(): lax.psum_scatter(line.step(frag_anchor - frag_local[0]), 'island', scatte...  6.9 us
    add x1, other arithmetic, per_device(): new_momentum = OUTER_MOMENT * momentum_rows + outer_grad  6.09 us
    unnamed x41, local copies, waits for them, and re-layouts  5.34 us
  transfers between devices with their start and end apart: 29, of which 9 were waited for; matrix products, arithmetic and copies ran while one was open for 25% of the time, Pallas kernels for 9%

profile of v2, /device:TPU:1, one launch (start us, length us, event | category | flops | bytes accessed | tf_op | source)
XLA Modules:
  0.0 200.5 jit_solution(13243057259280145931)
XLA Ops:
  7.4 1.8 dynamic-slice_bitcast_fusion.1
  10.3 1.4 collective-permute-start.1
  11.8 1.7 bitcast_subtract_fusion
  13.7 2.1 %collective-permute-done.1 = bf16[512,1024]{1,0:T(8,128)(2,1)} collective-permute-done((bf16[512,1024]{1,0:T(8,128)(2,1)}, bf16[512,1024]{1,0:T(8,128)(2,1)}, u32[]{:S(2)}, u32[]{:S(2)}) %collective-permute-start.1) | collective-permute-done | bytes 1048608 | tf_op jit(solution)/shard_map/ppermute | solution.py:52
  16.1 2.0 %pad_maximum_fusion.refs_2_.refs_0_ = bf16[1024,1024]{1,0:T(8,128)(2,1)S(1)} fusion(bf16[512,1024]{1,0:T(8,128)(2,1)} %collective-permute-done.1, bf16[512,512]{1,0:T(8,128)(2,1)S(1)} %get-tuple-element.180, bf16[512,512]{1,0:T(8,128)(2,1)S(1)} %get-tuple-element.177), kind=kLoop, calls=%fused_computation.13 | loop fusion | flops 6291456 | bytes 4194304 | tf_op jit(solution)/shard_map/concatenate | solution.py:260
  18.1 1.9 convolution_convert_fusion
  20.0 1.9 convolution_convert_fusion.1
  21.9 1.5 convolution_convert_fusion.2
  23.4 2.1 %shard_map.127 = (bf16[512,3072]{1,0:T(8,128)(2,1)S(1)}, bf16[1024,3072]{1,0:T(8,128)(2,1)S(1)}) custom-call(s32[12]{0:T(128)S(1)} %concatenate.44.where, bf16[512,8192]{1,0:T(8,128)(2,1)S(1)} %bitcast.70, bf16[512,8192]{1,0:T(8,128)(2,1)S(1)} %bitcast.71), custom_call_target="tpu_custom_call" | custom-call | flops 1 | bytes 1 | tf_op jit(solution)/shard_map/pallas_call | solution.py:74
  27.3 1.4 collective-permute-start.4
  28.8 2.7 %collective-permute-start.5 = (bf16[512,384]{1,0:T(8,128)(2,1)}, bf16[512,384]{1,0:T(8,128)(2,1)}, u32[]{:S(2)}, u32[]{:S(2)}) collective-permute-start(bf16[512,384]{1,0:T(8,128)(2,1)} %convolution_convert_fusion.2), channel_id=1, source_target_pairs={{0,8},{1,9},{2,10},{3,11},{4,12},{5,13},{6,14},{7,15},{8,0},{9,1},... | collective-permute-start | bytes 1179656 | tf_op jit(solution)/shard_map/ppermute | solution.py:52
  33.0 3.1 %fusion.2 = bf16[1536,384]{1,0:T(8,128)(2,1)} fusion(bf16[1024,384]{1,0:T(8,128)(2,1)S(1)} %pad_maximum_fusion.6, bf16[1024,3072]{1,0:T(8,128)(2,1)S(1)} %shard_map.128.refs_0_.refs_1_.refs_2_.refs_3_), kind=kOutput, calls=%fused_computation.4 | convolution fusion | flops 1208549376 | bytes 5111808 | tf_op jit(solution)/shard_map/dot_general | solution.py:264
  36.1 1.9 fusion.19
  38.0 1.5 copy-done.8
  39.5 6.9 %reduce-scatter.2.cloned.1.call-done = f32[128,1024]{1,0:T(8,128)} async-done(((f32[512,1024]{1,0:T(8,128)}), f32[128,1024]{1,0:T(8,128)}) %reduce-scatter.2.cloned.1.call-update) | async-done | bytes 524304 | tf_op jit(solution)/shard_map/reduce_scatter | solution.py:251
  46.4 3.8 %fusion.17 = f32[1024,640]{1,0:T(8,128)S(1)} fusion(bf16[1024,640]{1,0:T(8,128)(2,1)} %copy-done.10, bf16[1024,3072]{1,0:T(8,128)(2,1)} %copy-done), kind=kOutput, calls=%fused_computation.29 | convolution fusion | flops 1342177280 | bytes 6029312 | tf_op jit(solution)/shard_map/dot_general | solution.py:264
  50.3 2.0 add_convert_fusion.2
  52.3 1.6 add_convert_fusion
  55.5 1.5 collective-permute-start.7
  58.2 2.4 %collective-permute-start.10 = (bf16[1536,384]{1,0:T(8,128)(2,1)}, bf16[1536,384]{1,0:T(8,128)(2,1)}, u32[]{:S(2)}, u32[]{:S(2)}) collective-permute-start(bf16[1536,384]{1,0:T(8,128)(2,1)} %fusion.2), channel_id=1, source_target_pairs={{0,8},{1,9},{2,10},{3,11},{4,12},{5,13},{6,14},{7,15},{8,0},{9,1},... | collective-permute-start | bytes 3538952 | tf_op jit(solution)/shard_map/ppermute | solution.py:52
  60.6 8.6 %collective-permute-done.8 = f32[128,1024]{1,0:T(8,128)S(1)} collective-permute-done((f32[128,1024]{1,0:T(8,128)S(1)}, f32[128,1024]{1,0:T(8,128)S(1)}, u32[]{:S(2)}, u32[]{:S(2)}) %collective-permute-start.8) | collective-permute-done | bytes 524320 | tf_op jit(solution)/shard_map/ppermute | solution.py:289
  70.5 14.8 %collective-permute-done.6 = bf16[1024,640]{1,0:T(8,128)(2,1)S(1)} collective-permute-done((bf16[1024,640]{1,0:T(8,128)(2,1)S(1)}, bf16[1024,640]{1,0:T(8,128)(2,1)S(1)}, u32[]{:S(2)}, u32[]{:S(2)}) %collective-permute-start.6) | collective-permute-done | bytes 1310752 | tf_op jit(solution)/shard_map/ppermute | solution.py:52
  85.3 3.9 %fusion.24 = bf16[512,640]{1,0:T(8,128)(2,1)} fusion(bf16[1024,640]{1,0:T(8,128)(2,1)S(1)} %copy-done.11, bf16[1024,3072]{1,0:T(8,128)(2,1)} %copy-done, bf16[1024,640]{1,0:T(8,128)(2,1)S(1)} %collective-permute-done.7, bf16[1024,640]{1,0:T(8,128)(2,1)S(1)} %collective-permute-done.6), kind=kOutput, calls=%fused_computation.38 | convolution fusion | flops 672727040 | bytes 4325376 | tf_op jit(solution)/shard_map/dot_general | solution.py:264
  90.1 2.6 %collective-permute-start.9 = (bf16[512,640]{1,0:T(8,128)(2,1)}, bf16[512,640]{1,0:T(8,128)(2,1)}, u32[]{:S(2)}, u32[]{:S(2)}) collective-permute-start(bf16[512,640]{1,0:T(8,128)(2,1)} %fusion.24), channel_id=1, source_target_pairs={{0,8},{1,9},{2,10},{3,11},{4,12},{5,13},{6,14},{7,15},{8,0},{9,1},... | collective-permute-start | bytes 1966088 | tf_op jit(solution)/shard_map/ppermute | solution.py:52
  92.8 2.7 %fusion.22 = f32[512,640]{1,0:T(8,128)S(1)} fusion(bf16[1024,640]{1,0:T(8,128)(2,1)S(1)} %copy-done.12, bf16[1024,3072]{1,0:T(8,128)(2,1)} %copy-done, bf16[1024,640]{1,0:T(8,128)(2,1)} %copy-done.17, bf16[1024,640]{1,0:T(8,128)(2,1)} %copy-done.16), kind=kOutput, calls=%fused_computation.35 | convolution fusion | flops 672399360 | bytes 4980736 | tf_op jit(solution)/shard_map/dot_general | solution.py:264
  95.5 2.9 %fusion.15 = f32[1024,384]{1,0:T(8,128)S(1)} fusion(bf16[1024,384]{1,0:T(8,128)(2,1)S(1)} %copy-done.14, bf16[1024,3072]{1,0:T(8,128)(2,1)} %copy-done), kind=kOutput, calls=%fused_computation.27 | convolution fusion | flops 805306368 | bytes 4456448 | tf_op jit(solution)/shard_map/dot_general | solution.py:264
  98.4 2.0 fusion.26
  100.4 1.5 convert_add_fusion.2
  104.7 2.2 %collective-permute-start.14 = (bf16[512,384]{1,0:T(8,128)(2,1)S(1)}, bf16[512,384]{1,0:T(8,128)(2,1)S(1)}, u32[]{:S(2)}, u32[]{:S(2)}) collective-permute-start(bf16[512,384]{1,0:T(8,128)(2,1)S(1)} %pad_maximum_fusion.8), channel_id=1, source_target_pairs={{0,6},{1,7},{2,0},{3,1},{4,2},{5,3},{6,4},{7,5},{8,14},{9,15},{10,... | collective-permute-start | bytes 1179656 | tf_op jit(solution)/shard_map/ppermute | solution.py:52
  106.9 6.2 %collective-permute-done.13 = bf16[512,384]{1,0:T(8,128)(2,1)S(1)} collective-permute-done((bf16[512,384]{1,0:T(8,128)(2,1)S(1)}, bf16[512,384]{1,0:T(8,128)(2,1)S(1)}, u32[]{:S(2)}, u32[]{:S(2)}) %collective-permute-start.13) | collective-permute-done | bytes 393248 | tf_op jit(solution)/shard_map/ppermute | solution.py:52
  115.6 2.5 %pad_maximum_fusion.1 = (f32[512,1024]{1,0:T(8,128)S(1)}, bf16[512,1024]{1,0:T(8,128)(2,1)}) fusion(f32[512,384]{1,0:T(8,128)S(1)} %convert_add_fusion.1, f32[512,640]{1,0:T(8,128)S(1)} %convert_add_fusion, f32[1,512,1024]{2,1,0:T(8,128)S(1)} %copy-done.4, f32[1,512,1024]{2,1,0:T(8,128)S(1)} %copy-done.5, f32[1,512,1024]{2,1,0:T(8,128)S(1)} %copy-done.3), kind=kLoop, calls=%fused_computation.16 | loop fusion | flops 7864320 | bytes 11534336 | tf_op jit(solution)/shard_map/concatenate | solution.py:333
  118.2 2.7 %collective-permute-start.16 = (bf16[512,1024]{1,0:T(8,128)(2,1)}, bf16[512,1024]{1,0:T(8,128)(2,1)}, u32[]{:S(2)}, u32[]{:S(2)}) collective-permute-start(bf16[512,1024]{1,0:T(8,128)(2,1)} %get-tuple-element.137.refs_6_), channel_id=1, source_target_pairs={{0,6},{1,7},{2,0},{3,1},{4,2},{5,3},{6,4},{7,5},{8,14},{9,15},{10,... | collective-permute-start | bytes 3145736 | tf_op jit(solution)/shard_map/ppermute | solution.py:52
  121.6 4.1 %bitcast_subtract_fusion.1 = (f32[512,1024]{1,0:T(8,128)}, f32[512,1024]{1,0:T(8,128)}, f32[512,1024]{1,0:T(8,128)}) fusion(f32[1,512,1024]{2,1,0:T(8,128)S(1)} %copy-done.3, f32[512,1024]{1,0:T(8,128)S(1)} %get-tuple-element.136, f32[1,512,1024]{2,1,0:T(8,128)S(1)} %copy-done.4, f32[1,512,1024]{2,1,0:T(8,128)S(1)} %copy-done.5), kind=kLoop, calls=%fused_computation.20 | loop fusion | flops 6815744 | bytes 14680064 | tf_op jit(solution)/shard_map/sub | solution.py:329
  125.7 6.1 %multiply_add_fusion = (f32[512,1024]{1,0:T(8,128)}, f32[512,1024]{1,0:T(8,128)}) fusion(f32[512,1024]{1,0:T(8,128)} %param.15, f32[512,1024]{1,0:T(8,128)} %all-gather.2.cloned.1.call-done, f32[512,1024]{1,0:T(8,128)} %param.14), kind=kLoop, calls=%fused_computation.26 | loop fusion | flops 3670016 | bytes 10485760 | tf_op jit(solution)/shard_map/add | solution.py:341
  131.8 8.7 %collective-permute-done.15.near_dn.refs_5_ = bf16[512,1024]{1,0:T(8,128)(2,1)S(1)} collective-permute-done((bf16[512,1024]{1,0:T(8,128)(2,1)}, bf16[512,1024]{1,0:T(8,128)(2,1)S(1)}, u32[]{:S(2)}, u32[]{:S(2)}) %collective-permute-start.15) | collective-permute-done | bytes 1048608 | tf_op jit(solution)/shard_map/ppermute | solution.py:52
  140.5 2.4 %collective-permute-done.17.across.refs_7_ = bf16[512,1024]{1,0:T(8,128)(2,1)} collective-permute-done((bf16[512,1024]{1,0:T(8,128)(2,1)}, bf16[512,1024]{1,0:T(8,128)(2,1)}, u32[]{:S(2)}, u32[]{:S(2)}) %collective-permute-start.17) | collective-permute-done | bytes 1048608 | tf_op jit(solution)/shard_map/ppermute | solution.py:52
  142.9 1.7 shard_map.129
  145.8 2.7 %collective-permute-start.22 = (bf16[512,640]{1,0:T(8,128)(2,1)S(1)}, bf16[512,640]{1,0:T(8,128)(2,1)S(1)}, u32[]{:S(2)}, u32[]{:S(2)}) collective-permute-start(bf16[512,640]{1,0:T(8,128)(2,1)S(1)} %get-tuple-element.155), channel_id=1, source_target_pairs={{0,6},{1,7},{2,0},{3,1},{4,2},{5,3},{6,4},{7,5},{8,14},{9,15},{10,... | collective-permute-start | bytes 1966088 | tf_op jit(solution)/shard_map/ppermute | solution.py:52
  148.5 2.7 %collective-permute-start.20 = (bf16[256,1024]{1,0:T(8,128)(2,1)S(1)}, bf16[256,1024]{1,0:T(8,128)(2,1)S(1)}, u32[]{:S(2)}, u32[]{:S(2)}) collective-permute-start(bf16[256,1024]{1,0:T(8,128)(2,1)S(1)} %get-tuple-element.154), channel_id=1, source_target_pairs={{0,6},{1,7},{2,0},{3,1},{4,2},{5,3},{6,4},{7,5},{8,14},{9,15},{10,... | collective-permute-start | bytes 1572872 | tf_op jit(solution)/shard_map/ppermute | solution.py:52
  151.2 2.8 %copy-done.1 = bf16[1024,3072]{1,0:T(8,128)(2,1)S(1)} copy-done((bf16[1024,3072]{1,0:T(8,128)(2,1)S(1)}, bf16[1024,3072]{1,0:T(8,128)(2,1)}, u32[]{:S(2)}) %copy-start.1) | copy-done | bytes 6291480
  153.9 8.3 %shard_map.130.refs_8_ = f32[1024,1024]{1,0:T(8,128)S(1)} custom-call(s32[1]{0:T(128)} %constant.183.clone.1.where, bf16[1024,3072]{1,0:T(8,128)(2,1)S(1)} %copy-done.1, bf16[1024,3072]{1,0:T(8,128)(2,1)S(1)} %copy-done.1, bf16[1024,3072]{1,0:T(8,128)(2,1)S(1)} %copy-done.1, bf16[1024,3072]{1,0:T(8,128)(2,1)S(1)} %copy-done.1, ...), custom_call_target="tpu_custom_call" | custom-call | flops 1 | bytes 1 | tf_op jit(solution)/shard_map/pallas_call | solution.py:74
  162.2 6.9 %collective-permute-done.19 = bf16[256,1024]{1,0:T(8,128)(2,1)S(1)} collective-permute-done((bf16[256,1024]{1,0:T(8,128)(2,1)S(1)}, bf16[256,1024]{1,0:T(8,128)(2,1)S(1)}, u32[]{:S(2)}, u32[]{:S(2)}) %collective-permute-start.19) | collective-permute-done | bytes 524320 | tf_op jit(solution)/shard_map/ppermute | solution.py:52
  169.4 1.7 collective-permute-start.23
  171.1 2.7 %collective-permute-start.25 = (bf16[256,640]{1,0:T(8,128)(2,1)S(1)}, bf16[256,640]{1,0:T(8,128)(2,1)S(1)}, u32[]{:S(2)}, u32[]{:S(2)}) collective-permute-start(bf16[256,640]{1,0:T(8,128)(2,1)S(1)} %slice.155), channel_id=1, source_target_pairs={{0,6},{1,7},{2,0},{3,1},{4,2},{5,3},{6,4},{7,5},{8,14},{9,15},{10,... | collective-permute-start | bytes 983048 | tf_op jit(solution)/shard_map/ppermute | solution.py:52
  173.9 5.1 %shard_map.131.refs_3_ = f32[1024,1024]{1,0:T(8,128)S(1)} custom-call(s32[1]{0:T(128)} %constant.183.clone.1.where, bf16[1024,3072]{1,0:T(8,128)(2,1)S(1)} %copy-done.1, bf16[1024,3072]{1,0:T(8,128)(2,1)S(1)} %copy-done.1, bf16[1024,1024]{1,0:T(8,128)(2,1)S(1)} %pad_maximum_fusion.refs_2_.refs_0_, bf16[512,640]{1,0:T(8,128)(2,1)S(1)} %collective-permute-done.22.refs_3_, ...), custom_call_target="tpu_custom_call" | custom-call | flops 1 | bytes 1 | tf_op jit(solution)/shard_map/pallas_call | solution.py:74
  180.2 7.9 %collective-permute-start.26 = (f32[512,1024]{1,0:T(8,128)S(1)}, f32[512,1024]{1,0:T(8,128)S(1)}, u32[]{:S(2)}, u32[]{:S(2)}) collective-permute-start(f32[512,1024]{1,0:T(8,128)S(1)} %shard_map.133), channel_id=1, source_target_pairs={{0,1},{1,0},{2,3},{3,2},{4,5},{5,4},{6,7},{7,6},{8,9},{9,8},{10,11... | collective-permute-start | bytes 6291464 | tf_op jit(solution)/shard_map/ppermute | solution.py:52
  189.2 2.7 %collective-permute-done.26 = f32[512,1024]{1,0:T(8,128)S(1)} collective-permute-done((f32[512,1024]{1,0:T(8,128)S(1)}, f32[512,1024]{1,0:T(8,128)S(1)}, u32[]{:S(2)}, u32[]{:S(2)}) %collective-permute-start.26) | collective-permute-done | bytes 2097184 | tf_op jit(solution)/shard_map/ppermute | solution.py:52
  191.9 1.7 add_bitcast_fusion
  (107 shorter events, 19.7 us)
Async XLA Ops:
  7.2 39.2 %reduce-scatter.2.cloned.1.call-start = ((), (), s32[]{:S(2)}) async-start(), calls=%async_computation.1 | async-start | bytes 2621440 | tf_op jit(solution)/shard_map/reduce_scatter | solution.py:251
  7.4 4.4 %copy-start.6 = (bf16[1,512,1024]{2,1,0:T(8,128)(2,1)S(1)}, bf16[1,512,1024]{2,1,0:T(8,128)(2,1)}, u32[]{:S(2)}) copy-start(bf16[1,512,1024]{2,1,0:T(8,128)(2,1)} %param.9) | copy-start | bytes 3145732
  7.4 4.4 %copy-start.7 = (f32[1,512,1024]{2,1,0:T(8,128)S(1)}, f32[1,512,1024]{2,1,0:T(8,128)}, u32[]{:S(2)}) copy-start(f32[1,512,1024]{2,1,0:T(8,128)} %param.13) | copy-start | bytes 6291460
  9.2 2.5 %copy-start.2 = (f32[512,1024]{1,0:T(8,128)S(1)}, f32[512,1024]{1,0:T(8,128)}, u32[]{:S(2)}) copy-start(f32[512,1024]{1,0:T(8,128)} %param.14) | copy-start | bytes 6291460
  10.3 5.5 %collective-permute-start.1 = (bf16[512,1024]{1,0:T(8,128)(2,1)}, bf16[512,1024]{1,0:T(8,128)(2,1)}, u32[]{:S(2)}, u32[]{:S(2)}) collective-permute-start(bf16[512,1024]{1,0:T(8,128)(2,1)} %pad_maximum_fusion.4), channel_id=1, source_target_pairs={{0,1},{1,0},{2,3},{3,2},{4,5},{5,4},{6,7},{7,6},{8,9},{9,8},{10,11... | collective-permute-start | bytes 3145736 | tf_op jit(solution)/shard_map/ppermute | solution.py:52
  11.7 4.1 %collective-permute-start = (bf16[512,1024]{1,0:T(8,128)(2,1)S(1)}, bf16[512,1024]{1,0:T(8,128)(2,1)S(1)}, u32[]{:S(2)}, u32[]{:S(2)}) collective-permute-start(bf16[512,1024]{1,0:T(8,128)(2,1)S(1)} %bitcast.72), channel_id=1, source_target_pairs={{0,1},{1,0},{2,3},{3,2},{4,5},{5,4},{6,7},{7,6},{8,9},{9,8},{10,11... | collective-permute-start | bytes 3145736 | tf_op jit(solution)/shard_map/ppermute | solution.py:52
  13.5 112.2 %all-gather.2.cloned.1.call-start = ((), (), s32[]{:S(2)}) async-start(), calls=%async_computation.2 | async-start | bytes 2621440 | tf_op jit(solution)/shard_map/all_gather | solution.py:309
  15.9 17.1 %copy-start.13 = (bf16[1024,384]{1,0:T(8,128)(2,1)}, bf16[1024,384]{1,0:T(8,128)(2,1)S(1)}, u32[]{:S(2)}) copy-start(bf16[1024,384]{1,0:T(8,128)(2,1)S(1)} %pad_maximum_fusion.6) | copy-start | bytes 2359300
  16.1 20.0 %copy-start.10 = (bf16[1024,640]{1,0:T(8,128)(2,1)}, bf16[1024,640]{1,0:T(8,128)(2,1)S(1)}, u32[]{:S(2)}) copy-start(bf16[1024,640]{1,0:T(8,128)(2,1)S(1)} %fusion.25) | copy-start | bytes 3932164
  18.1 5.3 %slice-start = ((s8[8388608]{0:T(1024)(128)(4,1)}), s8[4194304]{0:T(1024)(128)(4,1)S(1)}, s32[]{:S(2)}) async-start(s8[8388608]{0:T(1024)(128)(4,1)} %bitcast.68), calls=%async_computation.3 | async-start | bytes 8388608
  20.0 3.4 %slice-start.1 = ((s8[8388608]{0:T(1024)(128)(4,1)}), s8[4194304]{0:T(1024)(128)(4,1)S(1)}, s32[]{:S(2)}) async-start(s8[8388608]{0:T(1024)(128)(4,1)} %bitcast.68), calls=%async_computation.4 | async-start | bytes 8388608
  25.5 6.8 %collective-permute-start.2 = (bf16[512,3072]{1,0:T(8,128)(2,1)S(1)}, bf16[512,3072]{1,0:T(8,128)(2,1)S(1)}, u32[]{:S(2)}, u32[]{:S(2)}) collective-permute-start(bf16[512,3072]{1,0:T(8,128)(2,1)S(1)} %get-tuple-element.99), channel_id=1, source_target_pairs={{0,1},{1,0},{2,3},{3,2},{4,5},{5,4},{6,7},{7,6},{8,9},{9,8},{10,11... | collective-permute-start | bytes 9437192 | tf_op jit(solution)/shard_map/ppermute | solution.py:52
  25.9 24.4 %collective-permute-start.3 = (bf16[512,640]{1,0:T(8,128)(2,1)}, bf16[512,640]{1,0:T(8,128)(2,1)}, u32[]{:S(2)}, u32[]{:S(2)}) collective-permute-start(bf16[512,640]{1,0:T(8,128)(2,1)} %convolution_convert_fusion), channel_id=1, source_target_pairs={{0,2},{1,3},{2,4},{3,5},{4,6},{5,7},{6,0},{7,1},{8,10},{9,11},{10,... | collective-permute-start | bytes 1966088 | tf_op jit(solution)/shard_map/ppermute | solution.py:52
  27.3 23.0 %collective-permute-start.4 = (bf16[512,640]{1,0:T(8,128)(2,1)}, bf16[512,640]{1,0:T(8,128)(2,1)}, u32[]{:S(2)}, u32[]{:S(2)}) collective-permute-start(bf16[512,640]{1,0:T(8,128)(2,1)} %convolution_convert_fusion.1), channel_id=1, source_target_pairs={{0,6},{1,7},{2,0},{3,1},{4,2},{5,3},{6,4},{7,5},{8,14},{9,15},{10,... | collective-permute-start | bytes 1966088 | tf_op jit(solution)/shard_map/ppermute | solution.py:52
  28.8 21.5 %collective-permute-start.5 = (bf16[512,384]{1,0:T(8,128)(2,1)}, bf16[512,384]{1,0:T(8,128)(2,1)}, u32[]{:S(2)}, u32[]{:S(2)}) collective-permute-start(bf16[512,384]{1,0:T(8,128)(2,1)} %convolution_convert_fusion.2), channel_id=1, source_target_pairs={{0,8},{1,9},{2,10},{3,11},{4,12},{5,13},{6,14},{7,15},{8,0},{9,1},... | collective-permute-start | bytes 1179656 | tf_op jit(solution)/shard_map/ppermute | solution.py:52
  33.0 3.1 %copy-start = (bf16[1024,3072]{1,0:T(8,128)(2,1)}, bf16[1024,3072]{1,0:T(8,128)(2,1)S(1)}, u32[]{:S(2)}) copy-start(bf16[1024,3072]{1,0:T(8,128)(2,1)S(1)} %shard_map.128.refs_0_.refs_1_.refs_2_.refs_3_) | copy-start | bytes 18874372
  50.2 2.1 %copy-start.9 = (f32[1024,640]{1,0:T(8,128)S(1)}, f32[1024,640]{1,0:T(8,128)}, u32[]{:S(2)}) copy-start(f32[1024,640]{1,0:T(8,128)} %copy-done.8) | copy-start | bytes 7864324
  53.9 3.0 %copy-start.15 = (f32[128,1024]{1,0:T(8,128)S(1)}, f32[128,1024]{1,0:T(8,128)}, u32[]{:S(2)}) copy-start(f32[128,1024]{1,0:T(8,128)} %reduce-scatter.2.cloned.1.call-done) | copy-start | bytes 1572868
  54.0 31.3 %copy-start.11 = (bf16[1024,640]{1,0:T(8,128)(2,1)S(1)}, bf16[1024,640]{1,0:T(8,128)(2,1)}, u32[]{:S(2)}) copy-start(bf16[1024,640]{1,0:T(8,128)(2,1)} %copy-done.10) | copy-start | bytes 3932164
  54.2 31.1 %collective-permute-start.6 = (bf16[1024,640]{1,0:T(8,128)(2,1)S(1)}, bf16[1024,640]{1,0:T(8,128)(2,1)S(1)}, u32[]{:S(2)}, u32[]{:S(2)}) collective-permute-start(bf16[1024,640]{1,0:T(8,128)(2,1)S(1)} %pad_maximum_fusion.2), channel_id=1, source_target_pairs={{0,2},{1,3},{2,4},{3,5},{4,6},{5,7},{6,0},{7,1},{8,10},{9,11},{10,... | collective-permute-start | bytes 3932168 | tf_op jit(solution)/shard_map/ppermute | solution.py:52
  55.5 29.8 %collective-permute-start.7 = (bf16[1024,640]{1,0:T(8,128)(2,1)S(1)}, bf16[1024,640]{1,0:T(8,128)(2,1)S(1)}, u32[]{:S(2)}, u32[]{:S(2)}) collective-permute-start(bf16[1024,640]{1,0:T(8,128)(2,1)S(1)} %pad_maximum_fusion.3), channel_id=1, source_target_pairs={{0,6},{1,7},{2,0},{3,1},{4,2},{5,3},{6,4},{7,5},{8,14},{9,15},{10,... | collective-permute-start | bytes 3932168 | tf_op jit(solution)/shard_map/ppermute | solution.py:52
  57.0 12.2 %collective-permute-start.8 = (f32[128,1024]{1,0:T(8,128)S(1)}, f32[128,1024]{1,0:T(8,128)S(1)}, u32[]{:S(2)}, u32[]{:S(2)}) collective-permute-start(f32[128,1024]{1,0:T(8,128)S(1)} %copy-done.15), channel_id=1, source_target_pairs={{0,16},{16,0},{32,48},{48,32},{64,80},{80,64},{96,112},{112,96},{1... | collective-permute-start | bytes 1572872 | tf_op jit(solution)/shard_map/ppermute | solution.py:289
  58.2 42.3 %collective-permute-start.10 = (bf16[1536,384]{1,0:T(8,128)(2,1)}, bf16[1536,384]{1,0:T(8,128)(2,1)}, u32[]{:S(2)}, u32[]{:S(2)}) collective-permute-start(bf16[1536,384]{1,0:T(8,128)(2,1)} %fusion.2), channel_id=1, source_target_pairs={{0,8},{1,9},{2,10},{3,11},{4,12},{5,13},{6,14},{7,15},{8,0},{9,1},... | collective-permute-start | bytes 3538952 | tf_op jit(solution)/shard_map/ppermute | solution.py:52
  60.5 39.8 %collective-permute-start.11 = (bf16[256,384]{1,0:T(8,128)(2,1)}, bf16[256,384]{1,0:T(8,128)(2,1)}, u32[]{:S(2)}, u32[]{:S(2)}) collective-permute-start(bf16[256,384]{1,0:T(8,128)(2,1)} %get-tuple-element.113), channel_id=1, source_target_pairs={{0,2},{1,3},{2,4},{3,5},{4,6},{5,7},{6,0},{7,1},{8,10},{9,11},{10,... | collective-permute-start | bytes 589832 | tf_op jit(solution)/shard_map/ppermute | solution.py:52
  69.2 31.2 %collective-permute-start.12 = (bf16[256,384]{1,0:T(8,128)(2,1)}, bf16[256,384]{1,0:T(8,128)(2,1)}, u32[]{:S(2)}, u32[]{:S(2)}) collective-permute-start(bf16[256,384]{1,0:T(8,128)(2,1)} %get-tuple-element.114), channel_id=1, source_target_pairs={{0,6},{1,7},{2,0},{3,1},{4,2},{5,3},{6,4},{7,5},{8,14},{9,15},{10,... | collective-permute-start | bytes 589832 | tf_op jit(solution)/shard_map/ppermute | solution.py:52
  85.3 4.0 %copy-start.16 = (bf16[1024,640]{1,0:T(8,128)(2,1)}, bf16[1024,640]{1,0:T(8,128)(2,1)S(1)}, u32[]{:S(2)}) copy-start(bf16[1024,640]{1,0:T(8,128)(2,1)S(1)} %collective-permute-done.6) | copy-start | bytes 3932164
  85.3 4.0 %copy-start.17 = (bf16[1024,640]{1,0:T(8,128)(2,1)}, bf16[1024,640]{1,0:T(8,128)(2,1)S(1)}, u32[]{:S(2)}) copy-start(bf16[1024,640]{1,0:T(8,128)(2,1)S(1)} %collective-permute-done.7) | copy-start | bytes 3932164
  89.3 3.5 %copy-start.12 = (bf16[1024,640]{1,0:T(8,128)(2,1)S(1)}, bf16[1024,640]{1,0:T(8,128)(2,1)}, u32[]{:S(2)}) copy-start(bf16[1024,640]{1,0:T(8,128)(2,1)} %copy-done.10) | copy-start | bytes 3932164
  90.1 23.0 %collective-permute-start.9 = (bf16[512,640]{1,0:T(8,128)(2,1)}, bf16[512,640]{1,0:T(8,128)(2,1)}, u32[]{:S(2)}, u32[]{:S(2)}) collective-permute-start(bf16[512,640]{1,0:T(8,128)(2,1)} %fusion.24), channel_id=1, source_target_pairs={{0,8},{1,9},{2,10},{3,11},{4,12},{5,13},{6,14},{7,15},{8,0},{9,1},... | collective-permute-start | bytes 1966088 | tf_op jit(solution)/shard_map/ppermute | solution.py:52
  92.8 2.7 %copy-start.14 = (bf16[1024,384]{1,0:T(8,128)(2,1)S(1)}, bf16[1024,384]{1,0:T(8,128)(2,1)}, u32[]{:S(2)}) copy-start(bf16[1024,384]{1,0:T(8,128)(2,1)} %copy-done.13) | copy-start | bytes 2359300
  104.1 10.6 %copy-start.5 = (f32[1,512,1024]{2,1,0:T(8,128)S(1)}, f32[1,512,1024]{2,1,0:T(8,128)}, u32[]{:S(2)}) copy-start(f32[1,512,1024]{2,1,0:T(8,128)} %param.11) | copy-start | bytes 6291460
  104.1 9.0 %collective-permute-start.13 = (bf16[512,384]{1,0:T(8,128)(2,1)S(1)}, bf16[512,384]{1,0:T(8,128)(2,1)S(1)}, u32[]{:S(2)}, u32[]{:S(2)}) collective-permute-start(bf16[512,384]{1,0:T(8,128)(2,1)S(1)} %pad_maximum_fusion.7), channel_id=1, source_target_pairs={{0,2},{1,3},{2,4},{3,5},{4,6},{5,7},{6,0},{7,1},{8,10},{9,11},{10,... | collective-permute-start | bytes 1179656 | tf_op jit(solution)/shard_map/ppermute | solution.py:52
  104.7 8.4 %collective-permute-start.14 = (bf16[512,384]{1,0:T(8,128)(2,1)S(1)}, bf16[512,384]{1,0:T(8,128)(2,1)S(1)}, u32[]{:S(2)}, u32[]{:S(2)}) collective-permute-start(bf16[512,384]{1,0:T(8,128)(2,1)S(1)} %pad_maximum_fusion.8), channel_id=1, source_target_pairs={{0,6},{1,7},{2,0},{3,1},{4,2},{5,3},{6,4},{7,5},{8,14},{9,15},{10,... | collective-permute-start | bytes 1179656 | tf_op jit(solution)/shard_map/ppermute | solution.py:52
  113.1 1.8 copy-start.4
  113.3 2.4 %copy-start.3 = (f32[1,512,1024]{2,1,0:T(8,128)S(1)}, f32[1,512,1024]{2,1,0:T(8,128)}, u32[]{:S(2)}) copy-start(f32[1,512,1024]{2,1,0:T(8,128)} %param.10) | copy-start | bytes 6291460
  118.1 22.4 %collective-permute-start.15 = (bf16[512,1024]{1,0:T(8,128)(2,1)}, bf16[512,1024]{1,0:T(8,128)(2,1)S(1)}, u32[]{:S(2)}, u32[]{:S(2)}) collective-permute-start(bf16[512,1024]{1,0:T(8,128)(2,1)} %get-tuple-element.137.refs_6_), channel_id=1, source_target_pairs={{0,2},{1,3},{2,4},{3,5},{4,6},{5,7},{6,0},{7,1},{8,10},{9,11},{10,... | collective-permute-start | bytes 3145736 | tf_op jit(solution)/shard_map/ppermute | solution.py:52
  118.2 22.4 %collective-permute-start.16 = (bf16[512,1024]{1,0:T(8,128)(2,1)}, bf16[512,1024]{1,0:T(8,128)(2,1)}, u32[]{:S(2)}, u32[]{:S(2)}) collective-permute-start(bf16[512,1024]{1,0:T(8,128)(2,1)} %get-tuple-element.137.refs_6_), channel_id=1, source_target_pairs={{0,6},{1,7},{2,0},{3,1},{4,2},{5,3},{6,4},{7,5},{8,14},{9,15},{10,... | collective-permute-start | bytes 3145736 | tf_op jit(solution)/shard_map/ppermute | solution.py:52
  120.8 22.1 %collective-permute-start.17 = (bf16[512,1024]{1,0:T(8,128)(2,1)}, bf16[512,1024]{1,0:T(8,128)(2,1)}, u32[]{:S(2)}, u32[]{:S(2)}) collective-permute-start(bf16[512,1024]{1,0:T(8,128)(2,1)} %get-tuple-element.137.refs_6_), channel_id=1, source_target_pairs={{0,8},{1,9},{2,10},{3,11},{4,12},{5,13},{6,14},{7,15},{8,0},{9,1},... | collective-permute-start | bytes 3145736 | tf_op jit(solution)/shard_map/ppermute | solution.py:52
  144.6 24.5 %collective-permute-start.18 = (bf16[1024,384]{1,0:T(8,128)(2,1)S(1)}, bf16[1024,384]{1,0:T(8,128)(2,1)S(1)}, u32[]{:S(2)}, u32[]{:S(2)}) collective-permute-start(bf16[1024,384]{1,0:T(8,128)(2,1)S(1)} %get-tuple-element.152), channel_id=1, source_target_pairs={{0,8},{1,9},{2,10},{3,11},{4,12},{5,13},{6,14},{7,15},{8,0},{9,1},... | collective-permute-start | bytes 2359304 | tf_op jit(solution)/shard_map/ppermute | solution.py:52
  145.8 23.4 %collective-permute-start.21 = (bf16[512,640]{1,0:T(8,128)(2,1)S(1)}, bf16[512,640]{1,0:T(8,128)(2,1)S(1)}, u32[]{:S(2)}, u32[]{:S(2)}) collective-permute-start(bf16[512,640]{1,0:T(8,128)(2,1)S(1)} %get-tuple-element.155), channel_id=1, source_target_pairs={{0,2},{1,3},{2,4},{3,5},{4,6},{5,7},{6,0},{7,1},{8,10},{9,11},{10,... | collective-permute-start | bytes 1966088 | tf_op jit(solution)/shard_map/ppermute | solution.py:52
  145.8 23.4 %collective-permute-start.22 = (bf16[512,640]{1,0:T(8,128)(2,1)S(1)}, bf16[512,640]{1,0:T(8,128)(2,1)S(1)}, u32[]{:S(2)}, u32[]{:S(2)}) collective-permute-start(bf16[512,640]{1,0:T(8,128)(2,1)S(1)} %get-tuple-element.155), channel_id=1, source_target_pairs={{0,6},{1,7},{2,0},{3,1},{4,2},{5,3},{6,4},{7,5},{8,14},{9,15},{10,... | collective-permute-start | bytes 1966088 | tf_op jit(solution)/shard_map/ppermute | solution.py:52
  148.5 20.7 %collective-permute-start.19 = (bf16[256,1024]{1,0:T(8,128)(2,1)S(1)}, bf16[256,1024]{1,0:T(8,128)(2,1)S(1)}, u32[]{:S(2)}, u32[]{:S(2)}) collective-permute-start(bf16[256,1024]{1,0:T(8,128)(2,1)S(1)} %get-tuple-element.153), channel_id=1, source_target_pairs={{0,2},{1,3},{2,4},{3,5},{4,6},{5,7},{6,0},{7,1},{8,10},{9,11},{10,... | collective-permute-start | bytes 1572872 | tf_op jit(solution)/shard_map/ppermute | solution.py:52
  148.5 20.7 %collective-permute-start.20 = (bf16[256,1024]{1,0:T(8,128)(2,1)S(1)}, bf16[256,1024]{1,0:T(8,128)(2,1)S(1)}, u32[]{:S(2)}, u32[]{:S(2)}) collective-permute-start(bf16[256,1024]{1,0:T(8,128)(2,1)S(1)} %get-tuple-element.154), channel_id=1, source_target_pairs={{0,6},{1,7},{2,0},{3,1},{4,2},{5,3},{6,4},{7,5},{8,14},{9,15},{10,... | collective-permute-start | bytes 1572872 | tf_op jit(solution)/shard_map/ppermute | solution.py:52
  151.2 2.8 %copy-start.1 = (bf16[1024,3072]{1,0:T(8,128)(2,1)S(1)}, bf16[1024,3072]{1,0:T(8,128)(2,1)}, u32[]{:S(2)}) copy-start(bf16[1024,3072]{1,0:T(8,128)(2,1)} %copy-done) | copy-start | bytes 18874372
  169.4 9.6 %collective-permute-start.23 = (bf16[512,384]{1,0:T(8,128)(2,1)S(1)}, bf16[512,384]{1,0:T(8,128)(2,1)S(1)}, u32[]{:S(2)}, u32[]{:S(2)}) collective-permute-start(bf16[512,384]{1,0:T(8,128)(2,1)S(1)} %pad_maximum_fusion.9), channel_id=1, source_target_pairs={{0,8},{1,9},{2,10},{3,11},{4,12},{5,13},{6,14},{7,15},{8,0},{9,1},... | collective-permute-start | bytes 1179656 | tf_op jit(solution)/shard_map/ppermute | solution.py:52
  171.1 7.9 %collective-permute-start.24 = (bf16[256,640]{1,0:T(8,128)(2,1)S(1)}, bf16[256,640]{1,0:T(8,128)(2,1)S(1)}, u32[]{:S(2)}, u32[]{:S(2)}) collective-permute-start(bf16[256,640]{1,0:T(8,128)(2,1)S(1)} %slice.154), channel_id=1, source_target_pairs={{0,2},{1,3},{2,4},{3,5},{4,6},{5,7},{6,0},{7,1},{8,10},{9,11},{10,... | collective-permute-start | bytes 983048 | tf_op jit(solution)/shard_map/ppermute | solution.py:52
  171.1 7.9 %collective-permute-start.25 = (bf16[256,640]{1,0:T(8,128)(2,1)S(1)}, bf16[256,640]{1,0:T(8,128)(2,1)S(1)}, u32[]{:S(2)}, u32[]{:S(2)}) collective-permute-start(bf16[256,640]{1,0:T(8,128)(2,1)S(1)} %slice.155), channel_id=1, source_target_pairs={{0,6},{1,7},{2,0},{3,1},{4,2},{5,3},{6,4},{7,5},{8,14},{9,15},{10,... | collective-permute-start | bytes 983048 | tf_op jit(solution)/shard_map/ppermute | solution.py:52
  180.2 11.7 %collective-permute-start.26 = (f32[512,1024]{1,0:T(8,128)S(1)}, f32[512,1024]{1,0:T(8,128)S(1)}, u32[]{:S(2)}, u32[]{:S(2)}) collective-permute-start(f32[512,1024]{1,0:T(8,128)S(1)} %shard_map.133), channel_id=1, source_target_pairs={{0,1},{1,0},{2,3},{3,2},{4,5},{5,4},{6,7},{7,6},{8,9},{9,8},{10,11... | collective-permute-start | bytes 6291464 | tf_op jit(solution)/shard_map/ppermute | solution.py:52
  (1 other events, 1.5 us)
Sparse Core Ops, SparseCore 0:
  13.6 32.7 reduce-scatter.1
  92.9 30.8 all-gather.1

commit v3 on v2

--- a/solution.py
+++ b/solution.py
@@ -300,6 +300,8 @@
     up_sent, down_sent, b_low, b_high = line.step(up_sent, down_sent, b_low, b_high)
     from_down, from_up = send(up_sent, UP), send(down_sent, DOWN)
     b_low, b_high = send(b_low, UP), send(b_high, DOWN)
+    share_other, rest_all = line.step(share_other, rest_all)
+    b_one, b_three = line.step(rest_term(0, 1, up_b), rest_term(4, 2, up_b))
 
     from_down, from_up, rest_all, share_other = line.step(from_down, from_up, rest_all, share_other)
     a_side = rest_term(2, 1, up_a) + wide(from_down[rows:]) + wide(from_up[:rows])
@@ -310,7 +312,6 @@
     from_down, from_up = line.hold(from_down, from_up)
     a_here = rest_term(5, 1, up_a) + wide(from_down[:rows]) + wide(from_up[rows:])
     a_here = line.step(a_here)
-    b_one, b_three = line.step(rest_term(0, 1, up_b), rest_term(4, 2, up_b))
 
     b_rest, b_low, b_high = line.step(b_rest, b_low, b_high)
     b_up = b_one + wide(b_rest[:rows])

time: 201 us -> 200 us (level)
  local copies, waits for them, and re-layouts: 7.67 us -> 9.76 us
    ppermute x26, waiting for transfers between devices: 43.9 us -> 40.9 us  [send(): return lax.ppermute(value, 'fsdp', pairs)]
    all_gather x1, waiting for transfers between devices: 0.01 us -> 2.14 us  [per_device(): lax.all_gather(share, 'island', axis=0, axis_index_groups=Z_GROUPS, tiled...]
    unnamed x41 -> x47, local copies, waits for them, and re-layouts: 5.34 us -> 7.44 us
  transfers between devices with their start and end apart: 29 -> 29, of which waited for: 9 -> 11; matrix products, arithmetic and copies ran while one was open for 25% -> 24% of each run, Pallas kernels for 9% -> 9%
where the time goes in v3:
time: 200 us
  waiting for transfers between devices  58.6 us (29%)
  starting transfers between devices  41.7 us (21%)
  other arithmetic  29.6 us (15%)
  matrix products  25.1 us (13%)
  Pallas kernels  20 us (10%)
  between operations  14.8 us (7%)
  local copies, waits for them, and re-layouts  9.76 us (5%)
    ppermute x26, waiting for transfers between devices, send(): return lax.ppermute(value, 'fsdp', pairs)  40.9 us
    ppermute x26, starting transfers between devices, send(): return lax.ppermute(value, 'fsdp', pairs)  40.4 us
    dot_general x11, matrix products, transposed(): lax.dot_general(lhs, upstream, (((0,), (0,)), ((), ())), preferred_elemen...  25.1 us
    pallas_call x7, Pallas kernels, kernel_call(): pl.pallas_call(body, out_shape=out_shape, grid_spec=pltpu.PrefetchScalarG...  20 us
    ppermute x1, waiting for transfers between devices, per_device(): share_other = lax.ppermute(share, 'island', X_LO)  8.62 us
    unnamed x47, local copies, waits for them, and re-layouts  7.44 us
    reduce_scatter x1, waiting for transfers between devices, per_device(): lax.psum_scatter(line.step(frag_anchor - frag_local[0]), 'island', scatte...  6.89 us
    add x1, other arithmetic, per_device(): new_momentum = OUTER_MOMENT * momentum_rows + outer_grad  6.09 us
  transfers between devices with their start and end apart: 29, of which 11 were waited for; matrix products, arithmetic and copies ran while one was open for 24% of the time, Pallas kernels for 9%

profile of v3, /device:TPU:1, one launch (start us, length us, event | category | flops | bytes accessed | tf_op | source)
XLA Modules:
  0.0 199.5 jit_solution(3700332892207702740)
XLA Ops:
  7.4 1.8 dynamic-slice_bitcast_fusion.1
  11.8 1.7 bitcast_subtract_fusion
  13.7 2.1 %collective-permute-done.1 = bf16[512,1024]{1,0:T(8,128)(2,1)} collective-permute-done((bf16[512,1024]{1,0:T(8,128)(2,1)}, bf16[512,1024]{1,0:T(8,128)(2,1)}, u32[]{:S(2)}, u32[]{:S(2)}) %collective-permute-start.1) | collective-permute-done | bytes 1048608 | tf_op jit(solution)/shard_map/ppermute | solution.py:52
  16.1 2.0 %pad_maximum_fusion.refs_2_.refs_0_ = bf16[1024,1024]{1,0:T(8,128)(2,1)S(1)} fusion(bf16[512,1024]{1,0:T(8,128)(2,1)} %collective-permute-done.1, bf16[512,512]{1,0:T(8,128)(2,1)S(1)} %get-tuple-element.184, bf16[512,512]{1,0:T(8,128)(2,1)S(1)} %get-tuple-element.181), kind=kLoop, calls=%fused_computation.13 | loop fusion | flops 6291456 | bytes 4194304 | tf_op jit(solution)/shard_map/concatenate | solution.py:260
  18.1 1.9 convolution_convert_fusion
  20.0 1.9 convolution_convert_fusion.1
  21.9 1.5 convolution_convert_fusion.2
  23.4 2.1 %shard_map.127 = (bf16[512,3072]{1,0:T(8,128)(2,1)S(1)}, bf16[1024,3072]{1,0:T(8,128)(2,1)S(1)}) custom-call(s32[12]{0:T(128)S(1)} %concatenate.44.where, bf16[512,8192]{1,0:T(8,128)(2,1)S(1)} %bitcast.72, bf16[512,8192]{1,0:T(8,128)(2,1)S(1)} %bitcast.73), custom_call_target="tpu_custom_call" | custom-call | flops 1 | bytes 1 | tf_op jit(solution)/shard_map/pallas_call | solution.py:74
  27.3 1.4 collective-permute-start.4
  28.8 2.7 %collective-permute-start.5 = (bf16[512,384]{1,0:T(8,128)(2,1)}, bf16[512,384]{1,0:T(8,128)(2,1)}, u32[]{:S(2)}, u32[]{:S(2)}) collective-permute-start(bf16[512,384]{1,0:T(8,128)(2,1)} %convolution_convert_fusion.2), channel_id=1, source_target_pairs={{0,8},{1,9},{2,10},{3,11},{4,12},{5,13},{6,14},{7,15},{8,0},{9,1},... | collective-permute-start | bytes 1179656 | tf_op jit(solution)/shard_map/ppermute | solution.py:52
  33.0 3.1 %fusion.2 = bf16[1536,384]{1,0:T(8,128)(2,1)} fusion(bf16[1024,384]{1,0:T(8,128)(2,1)S(1)} %pad_maximum_fusion.6, bf16[1024,3072]{1,0:T(8,128)(2,1)S(1)} %shard_map.128.refs_0_.refs_1_.refs_2_.refs_3_), kind=kOutput, calls=%fused_computation.4 | convolution fusion | flops 1208549376 | bytes 5111808 | tf_op jit(solution)/shard_map/dot_general | solution.py:264
  36.1 1.9 fusion.19
  38.0 1.5 copy-done.9
  39.5 6.9 %reduce-scatter.2.cloned.1.call-done = f32[128,1024]{1,0:T(8,128)} async-done(((f32[512,1024]{1,0:T(8,128)}), f32[128,1024]{1,0:T(8,128)}) %reduce-scatter.2.cloned.1.call-update) | async-done | bytes 524304 | tf_op jit(solution)/shard_map/reduce_scatter | solution.py:251
  46.4 3.8 %fusion.17 = f32[1024,640]{1,0:T(8,128)S(1)} fusion(bf16[1024,640]{1,0:T(8,128)(2,1)} %copy-done.11, bf16[1024,3072]{1,0:T(8,128)(2,1)} %copy-done), kind=kOutput, calls=%fused_computation.29 | convolution fusion | flops 1342177280 | bytes 6029312 | tf_op jit(solution)/shard_map/dot_general | solution.py:264
  50.3 2.0 %add_convert_fusion.2 = (bf16[256,384]{1,0:T(8,128)(2,1)}, bf16[256,384]{1,0:T(8,128)(2,1)}) fusion(f32[512,384]{1,0:T(8,128)S(1)} %fusion.30, bf16[512,384]{1,0:T(8,128)(2,1)} %collective-permute-done.5), kind=kLoop, calls=%fused_computation.79 | loop fusion | flops 589824 | bytes 1572864 | tf_op jit(solution)/shard_map/convert_element_type | solution.py:298
  52.4 1.8 add_convert_fusion
  55.7 1.5 collective-permute-start.7
  58.4 2.4 %collective-permute-start.10 = (bf16[1536,384]{1,0:T(8,128)(2,1)}, bf16[1536,384]{1,0:T(8,128)(2,1)}, u32[]{:S(2)}, u32[]{:S(2)}) collective-permute-start(bf16[1536,384]{1,0:T(8,128)(2,1)} %fusion.2), channel_id=1, source_target_pairs={{0,8},{1,9},{2,10},{3,11},{4,12},{5,13},{6,14},{7,15},{8,0},{9,1},... | collective-permute-start | bytes 3538952 | tf_op jit(solution)/shard_map/ppermute | solution.py:52
  60.8 8.6 %collective-permute-done.8 = f32[128,1024]{1,0:T(8,128)S(1)} collective-permute-done((f32[128,1024]{1,0:T(8,128)S(1)}, f32[128,1024]{1,0:T(8,128)S(1)}, u32[]{:S(2)}, u32[]{:S(2)}) %collective-permute-start.8) | collective-permute-done | bytes 524320 | tf_op jit(solution)/shard_map/ppermute | solution.py:289
  70.7 1.6 fusion.28
  72.3 2.4 %fusion.15 = f32[1024,384]{1,0:T(8,128)} fusion(bf16[1024,384]{1,0:T(8,128)(2,1)S(1)} %copy-done.14, bf16[1024,3072]{1,0:T(8,128)(2,1)S(1)} %bitcast.69), kind=kOutput, calls=%fused_computation.27 | convolution fusion | flops 805306368 | bytes 4456448 | tf_op jit(solution)/shard_map/dot_general | solution.py:264
  74.7 10.8 %collective-permute-done.6 = bf16[1024,640]{1,0:T(8,128)(2,1)S(1)} collective-permute-done((bf16[1024,640]{1,0:T(8,128)(2,1)S(1)}, bf16[1024,640]{1,0:T(8,128)(2,1)S(1)}, u32[]{:S(2)}, u32[]{:S(2)}) %collective-permute-start.6) | collective-permute-done | bytes 1310752 | tf_op jit(solution)/shard_map/ppermute | solution.py:52
  88.5 3.5 %fusion.24 = bf16[512,640]{1,0:T(8,128)(2,1)} fusion(bf16[1024,640]{1,0:T(8,128)(2,1)S(1)} %copy-done.12, bf16[1024,3072]{1,0:T(8,128)(2,1)} %copy-done, bf16[1024,640]{1,0:T(8,128)(2,1)} %copy-done.18, bf16[1024,640]{1,0:T(8,128)(2,1)} %copy-done.17), kind=kOutput, calls=%fused_computation.38 | convolution fusion | flops 672727040 | bytes 4325376 | tf_op jit(solution)/shard_map/dot_general | solution.py:264
  91.9 2.6 %collective-permute-start.9 = (bf16[512,640]{1,0:T(8,128)(2,1)}, bf16[512,640]{1,0:T(8,128)(2,1)}, u32[]{:S(2)}, u32[]{:S(2)}) collective-permute-start(bf16[512,640]{1,0:T(8,128)(2,1)} %fusion.24), channel_id=1, source_target_pairs={{0,8},{1,9},{2,10},{3,11},{4,12},{5,13},{6,14},{7,15},{8,0},{9,1},... | collective-permute-start | bytes 1966088 | tf_op jit(solution)/shard_map/ppermute | solution.py:52
  94.6 2.8 %fusion.22 = f32[512,640]{1,0:T(8,128)S(1)} fusion(bf16[1024,640]{1,0:T(8,128)(2,1)S(1)} %copy-done.12, bf16[1024,3072]{1,0:T(8,128)(2,1)} %copy-done, bf16[1024,640]{1,0:T(8,128)(2,1)} %copy-done.18, bf16[1024,640]{1,0:T(8,128)(2,1)} %copy-done.17), kind=kOutput, calls=%fused_computation.35 | convolution fusion | flops 672399360 | bytes 4980736 | tf_op jit(solution)/shard_map/dot_general | solution.py:264
  97.4 1.5 convert_add_fusion.2
  101.3 2.6 %collective-permute-start.14 = (bf16[512,384]{1,0:T(8,128)(2,1)S(1)}, bf16[512,384]{1,0:T(8,128)(2,1)S(1)}, u32[]{:S(2)}, u32[]{:S(2)}) collective-permute-start(bf16[512,384]{1,0:T(8,128)(2,1)S(1)} %pad_maximum_fusion.8), channel_id=1, source_target_pairs={{0,6},{1,7},{2,0},{3,1},{4,2},{5,3},{6,4},{7,5},{8,14},{9,15},{10,... | collective-permute-start | bytes 1179656 | tf_op jit(solution)/shard_map/ppermute | solution.py:52
  103.8 5.9 %collective-permute-done.13 = bf16[512,384]{1,0:T(8,128)(2,1)S(1)} collective-permute-done((bf16[512,384]{1,0:T(8,128)(2,1)S(1)}, bf16[512,384]{1,0:T(8,128)(2,1)S(1)}, u32[]{:S(2)}, u32[]{:S(2)}) %collective-permute-start.13) | collective-permute-done | bytes 393248 | tf_op jit(solution)/shard_map/ppermute | solution.py:52
  113.4 2.5 %pad_maximum_fusion.1 = (f32[512,1024]{1,0:T(8,128)S(1)}, bf16[512,1024]{1,0:T(8,128)(2,1)}) fusion(f32[512,384]{1,0:T(8,128)S(1)} %convert_add_fusion.1, f32[512,640]{1,0:T(8,128)S(1)} %convert_add_fusion, f32[1,512,1024]{2,1,0:T(8,128)S(1)} %copy-done.4, f32[1,512,1024]{2,1,0:T(8,128)S(1)} %copy-done.5, f32[1,512,1024]{2,1,0:T(8,128)S(1)} %copy-done.3), kind=kLoop, calls=%fused_computation.16 | loop fusion | flops 7864320 | bytes 11534336 | tf_op jit(solution)/shard_map/concatenate | solution.py:334
  116.0 2.7 %collective-permute-start.16 = (bf16[512,1024]{1,0:T(8,128)(2,1)}, bf16[512,1024]{1,0:T(8,128)(2,1)}, u32[]{:S(2)}, u32[]{:S(2)}) collective-permute-start(bf16[512,1024]{1,0:T(8,128)(2,1)} %get-tuple-element.141.refs_6_), channel_id=1, source_target_pairs={{0,6},{1,7},{2,0},{3,1},{4,2},{5,3},{6,4},{7,5},{8,14},{9,15},{10,... | collective-permute-start | bytes 3145736 | tf_op jit(solution)/shard_map/ppermute | solution.py:52
  118.6 4.1 %bitcast_subtract_fusion.1 = (f32[512,1024]{1,0:T(8,128)}, f32[512,1024]{1,0:T(8,128)}, f32[512,1024]{1,0:T(8,128)}) fusion(f32[1,512,1024]{2,1,0:T(8,128)S(1)} %copy-done.3, f32[512,1024]{1,0:T(8,128)S(1)} %get-tuple-element.140, f32[1,512,1024]{2,1,0:T(8,128)S(1)} %copy-done.4, f32[1,512,1024]{2,1,0:T(8,128)S(1)} %copy-done.5), kind=kLoop, calls=%fused_computation.20 | loop fusion | flops 6815744 | bytes 14680064 | tf_op jit(solution)/shard_map/sub | solution.py:330
  122.7 2.1 %all-gather.2.cloned.1.call-done = f32[512,1024]{1,0:T(8,128)} async-done(((f32[128,1024]{1,0:T(8,128)}), f32[512,1024]{1,0:T(8,128)}) %all-gather.2.cloned.1.call-update) | async-done | bytes 2097168 | tf_op jit(solution)/shard_map/all_gather | solution.py:311
  124.9 6.1 %multiply_add_fusion = (f32[512,1024]{1,0:T(8,128)}, f32[512,1024]{1,0:T(8,128)}) fusion(f32[512,1024]{1,0:T(8,128)} %param.15, f32[512,1024]{1,0:T(8,128)} %all-gather.2.cloned.1.call-done, f32[512,1024]{1,0:T(8,128)} %param.14), kind=kLoop, calls=%fused_computation.26 | loop fusion | flops 3670016 | bytes 10485760 | tf_op jit(solution)/shard_map/add | solution.py:342
  131.0 8.2 %collective-permute-done.15.near_dn.refs_5_ = bf16[512,1024]{1,0:T(8,128)(2,1)S(1)} collective-permute-done((bf16[512,1024]{1,0:T(8,128)(2,1)}, bf16[512,1024]{1,0:T(8,128)(2,1)S(1)}, u32[]{:S(2)}, u32[]{:S(2)}) %collective-permute-start.15) | collective-permute-done | bytes 1048608 | tf_op jit(solution)/shard_map/ppermute | solution.py:52
  139.2 2.4 %collective-permute-done.17.across.refs_7_ = bf16[512,1024]{1,0:T(8,128)(2,1)} collective-permute-done((bf16[512,1024]{1,0:T(8,128)(2,1)}, bf16[512,1024]{1,0:T(8,128)(2,1)}, u32[]{:S(2)}, u32[]{:S(2)}) %collective-permute-start.17) | collective-permute-done | bytes 1048608 | tf_op jit(solution)/shard_map/ppermute | solution.py:52
  141.6 1.7 shard_map.129
  143.5 2.7 %collective-permute-start.22 = (bf16[512,640]{1,0:T(8,128)(2,1)S(1)}, bf16[512,640]{1,0:T(8,128)(2,1)S(1)}, u32[]{:S(2)}, u32[]{:S(2)}) collective-permute-start(bf16[512,640]{1,0:T(8,128)(2,1)S(1)} %get-tuple-element.159), channel_id=1, source_target_pairs={{0,6},{1,7},{2,0},{3,1},{4,2},{5,3},{6,4},{7,5},{8,14},{9,15},{10,... | collective-permute-start | bytes 1966088 | tf_op jit(solution)/shard_map/ppermute | solution.py:52
  146.2 2.7 %collective-permute-start.20 = (bf16[256,1024]{1,0:T(8,128)(2,1)S(1)}, bf16[256,1024]{1,0:T(8,128)(2,1)S(1)}, u32[]{:S(2)}, u32[]{:S(2)}) collective-permute-start(bf16[256,1024]{1,0:T(8,128)(2,1)S(1)} %get-tuple-element.158), channel_id=1, source_target_pairs={{0,6},{1,7},{2,0},{3,1},{4,2},{5,3},{6,4},{7,5},{8,14},{9,15},{10,... | collective-permute-start | bytes 1572872 | tf_op jit(solution)/shard_map/ppermute | solution.py:52
  148.8 2.8 %copy-done.1 = bf16[1024,3072]{1,0:T(8,128)(2,1)S(1)} copy-done((bf16[1024,3072]{1,0:T(8,128)(2,1)S(1)}, bf16[1024,3072]{1,0:T(8,128)(2,1)}, u32[]{:S(2)}) %copy-start.1) | copy-done | bytes 6291480
  151.6 8.3 %shard_map.130.refs_8_ = f32[1024,1024]{1,0:T(8,128)S(1)} custom-call(s32[1]{0:T(128)} %constant.183.clone.1.where, bf16[1024,3072]{1,0:T(8,128)(2,1)S(1)} %copy-done.1, bf16[1024,3072]{1,0:T(8,128)(2,1)S(1)} %copy-done.1, bf16[1024,3072]{1,0:T(8,128)(2,1)S(1)} %copy-done.1, bf16[1024,3072]{1,0:T(8,128)(2,1)S(1)} %copy-done.1, ...), custom_call_target="tpu_custom_call" | custom-call | flops 1 | bytes 1 | tf_op jit(solution)/shard_map/pallas_call | solution.py:74
  159.9 7.5 %collective-permute-done.19 = bf16[256,1024]{1,0:T(8,128)(2,1)S(1)} collective-permute-done((bf16[256,1024]{1,0:T(8,128)(2,1)S(1)}, bf16[256,1024]{1,0:T(8,128)(2,1)S(1)}, u32[]{:S(2)}, u32[]{:S(2)}) %collective-permute-start.19) | collective-permute-done | bytes 524320 | tf_op jit(solution)/shard_map/ppermute | solution.py:52
  167.7 2.9 %collective-permute-start.23 = (bf16[512,384]{1,0:T(8,128)(2,1)S(1)}, bf16[512,384]{1,0:T(8,128)(2,1)S(1)}, u32[]{:S(2)}, u32[]{:S(2)}) collective-permute-start(bf16[512,384]{1,0:T(8,128)(2,1)S(1)} %pad_maximum_fusion.9), channel_id=1, source_target_pairs={{0,8},{1,9},{2,10},{3,11},{4,12},{5,13},{6,14},{7,15},{8,0},{9,1},... | collective-permute-start | bytes 1179656 | tf_op jit(solution)/shard_map/ppermute | solution.py:52
  170.6 2.7 %collective-permute-start.25 = (bf16[256,640]{1,0:T(8,128)(2,1)S(1)}, bf16[256,640]{1,0:T(8,128)(2,1)S(1)}, u32[]{:S(2)}, u32[]{:S(2)}) collective-permute-start(bf16[256,640]{1,0:T(8,128)(2,1)S(1)} %slice.155), channel_id=1, source_target_pairs={{0,6},{1,7},{2,0},{3,1},{4,2},{5,3},{6,4},{7,5},{8,14},{9,15},{10,... | collective-permute-start | bytes 983048 | tf_op jit(solution)/shard_map/ppermute | solution.py:52
  173.4 5.1 %shard_map.131.refs_3_ = f32[1024,1024]{1,0:T(8,128)S(1)} custom-call(s32[1]{0:T(128)} %constant.183.clone.1.where, bf16[1024,3072]{1,0:T(8,128)(2,1)S(1)} %copy-done.1, bf16[1024,3072]{1,0:T(8,128)(2,1)S(1)} %copy-done.1, bf16[1024,1024]{1,0:T(8,128)(2,1)S(1)} %pad_maximum_fusion.refs_2_.refs_0_, bf16[512,640]{1,0:T(8,128)(2,1)S(1)} %collective-permute-done.22.refs_3_, ...), custom_call_target="tpu_custom_call" | custom-call | flops 1 | bytes 1 | tf_op jit(solution)/shard_map/pallas_call | solution.py:74
  179.7 7.4 %collective-permute-start.26 = (f32[512,1024]{1,0:T(8,128)S(1)}, f32[512,1024]{1,0:T(8,128)S(1)}, u32[]{:S(2)}, u32[]{:S(2)}) collective-permute-start(f32[512,1024]{1,0:T(8,128)S(1)} %shard_map.133), channel_id=1, source_target_pairs={{0,1},{1,0},{2,3},{3,2},{4,5},{5,4},{6,7},{7,6},{8,9},{9,8},{10,11... | collective-permute-start | bytes 6291464 | tf_op jit(solution)/shard_map/ppermute | solution.py:52
  188.2 2.7 %collective-permute-done.26 = f32[512,1024]{1,0:T(8,128)S(1)} collective-permute-done((f32[512,1024]{1,0:T(8,128)S(1)}, f32[512,1024]{1,0:T(8,128)S(1)}, u32[]{:S(2)}, u32[]{:S(2)}) %collective-permute-start.26) | collective-permute-done | bytes 2097184 | tf_op jit(solution)/shard_map/ppermute | solution.py:52
  190.9 1.7 add_bitcast_fusion
  (114 shorter events, 22.1 us)
Async XLA Ops:
  7.2 39.2 %reduce-scatter.2.cloned.1.call-start = ((), (), s32[]{:S(2)}) async-start(), calls=%async_computation.1 | async-start | bytes 2621440 | tf_op jit(solution)/shard_map/reduce_scatter | solution.py:251
  7.4 4.4 %copy-start.6 = (bf16[1,512,1024]{2,1,0:T(8,128)(2,1)S(1)}, bf16[1,512,1024]{2,1,0:T(8,128)(2,1)}, u32[]{:S(2)}) copy-start(bf16[1,512,1024]{2,1,0:T(8,128)(2,1)} %param.9) | copy-start | bytes 3145732
  7.4 4.4 %copy-start.7 = (f32[1,512,1024]{2,1,0:T(8,128)S(1)}, f32[1,512,1024]{2,1,0:T(8,128)}, u32[]{:S(2)}) copy-start(f32[1,512,1024]{2,1,0:T(8,128)} %param.13) | copy-start | bytes 6291460
  9.2 2.5 %copy-start.2 = (f32[512,1024]{1,0:T(8,128)S(1)}, f32[512,1024]{1,0:T(8,128)}, u32[]{:S(2)}) copy-start(f32[512,1024]{1,0:T(8,128)} %param.14) | copy-start | bytes 6291460
  10.3 5.5 %collective-permute-start.1 = (bf16[512,1024]{1,0:T(8,128)(2,1)}, bf16[512,1024]{1,0:T(8,128)(2,1)}, u32[]{:S(2)}, u32[]{:S(2)}) collective-permute-start(bf16[512,1024]{1,0:T(8,128)(2,1)} %pad_maximum_fusion.4), channel_id=1, source_target_pairs={{0,1},{1,0},{2,3},{3,2},{4,5},{5,4},{6,7},{7,6},{8,9},{9,8},{10,11... | collective-permute-start | bytes 3145736 | tf_op jit(solution)/shard_map/ppermute | solution.py:52
  11.7 4.1 %collective-permute-start = (bf16[512,1024]{1,0:T(8,128)(2,1)S(1)}, bf16[512,1024]{1,0:T(8,128)(2,1)S(1)}, u32[]{:S(2)}, u32[]{:S(2)}) collective-permute-start(bf16[512,1024]{1,0:T(8,128)(2,1)S(1)} %bitcast.74), channel_id=1, source_target_pairs={{0,1},{1,0},{2,3},{3,2},{4,5},{5,4},{6,7},{7,6},{8,9},{9,8},{10,11... | collective-permute-start | bytes 3145736 | tf_op jit(solution)/shard_map/ppermute | solution.py:52
  13.5 111.4 %all-gather.2.cloned.1.call-start = ((), (), s32[]{:S(2)}) async-start(), calls=%async_computation.2 | async-start | bytes 2621440 | tf_op jit(solution)/shard_map/all_gather | solution.py:311
  15.9 17.1 %copy-start.13 = (bf16[1024,384]{1,0:T(8,128)(2,1)}, bf16[1024,384]{1,0:T(8,128)(2,1)S(1)}, u32[]{:S(2)}) copy-start(bf16[1024,384]{1,0:T(8,128)(2,1)S(1)} %pad_maximum_fusion.6) | copy-start | bytes 2359300
  16.1 20.0 %copy-start.11 = (bf16[1024,640]{1,0:T(8,128)(2,1)}, bf16[1024,640]{1,0:T(8,128)(2,1)S(1)}, u32[]{:S(2)}) copy-start(bf16[1024,640]{1,0:T(8,128)(2,1)S(1)} %fusion.25) | copy-start | bytes 3932164
  18.1 5.3 %slice-start.2 = ((s8[8388608]{0:T(1024)(128)(4,1)}), s8[4194304]{0:T(1024)(128)(4,1)S(1)}, s32[]{:S(2)}) async-start(s8[8388608]{0:T(1024)(128)(4,1)} %bitcast.70), calls=%async_computation.5 | async-start | bytes 8388608
  20.0 3.4 %slice-start.3 = ((s8[8388608]{0:T(1024)(128)(4,1)}), s8[4194304]{0:T(1024)(128)(4,1)S(1)}, s32[]{:S(2)}) async-start(s8[8388608]{0:T(1024)(128)(4,1)} %bitcast.70), calls=%async_computation.6 | async-start | bytes 8388608
  25.5 6.8 %collective-permute-start.2 = (bf16[512,3072]{1,0:T(8,128)(2,1)S(1)}, bf16[512,3072]{1,0:T(8,128)(2,1)S(1)}, u32[]{:S(2)}, u32[]{:S(2)}) collective-permute-start(bf16[512,3072]{1,0:T(8,128)(2,1)S(1)} %get-tuple-element.101), channel_id=1, source_target_pairs={{0,1},{1,0},{2,3},{3,2},{4,5},{5,4},{6,7},{7,6},{8,9},{9,8},{10,11... | collective-permute-start | bytes 9437192 | tf_op jit(solution)/shard_map/ppermute | solution.py:52
  25.9 24.4 %collective-permute-start.3 = (bf16[512,640]{1,0:T(8,128)(2,1)}, bf16[512,640]{1,0:T(8,128)(2,1)}, u32[]{:S(2)}, u32[]{:S(2)}) collective-permute-start(bf16[512,640]{1,0:T(8,128)(2,1)} %convolution_convert_fusion), channel_id=1, source_target_pairs={{0,2},{1,3},{2,4},{3,5},{4,6},{5,7},{6,0},{7,1},{8,10},{9,11},{10,... | collective-permute-start | bytes 1966088 | tf_op jit(solution)/shard_map/ppermute | solution.py:52
  27.3 23.0 %collective-permute-start.4 = (bf16[512,640]{1,0:T(8,128)(2,1)}, bf16[512,640]{1,0:T(8,128)(2,1)}, u32[]{:S(2)}, u32[]{:S(2)}) collective-permute-start(bf16[512,640]{1,0:T(8,128)(2,1)} %convolution_convert_fusion.1), channel_id=1, source_target_pairs={{0,6},{1,7},{2,0},{3,1},{4,2},{5,3},{6,4},{7,5},{8,14},{9,15},{10,... | collective-permute-start | bytes 1966088 | tf_op jit(solution)/shard_map/ppermute | solution.py:52
  28.8 21.5 %collective-permute-start.5 = (bf16[512,384]{1,0:T(8,128)(2,1)}, bf16[512,384]{1,0:T(8,128)(2,1)}, u32[]{:S(2)}, u32[]{:S(2)}) collective-permute-start(bf16[512,384]{1,0:T(8,128)(2,1)} %convolution_convert_fusion.2), channel_id=1, source_target_pairs={{0,8},{1,9},{2,10},{3,11},{4,12},{5,13},{6,14},{7,15},{8,0},{9,1},... | collective-permute-start | bytes 1179656 | tf_op jit(solution)/shard_map/ppermute | solution.py:52
  33.0 3.1 %copy-start = (bf16[1024,3072]{1,0:T(8,128)(2,1)}, bf16[1024,3072]{1,0:T(8,128)(2,1)S(1)}, u32[]{:S(2)}) copy-start(bf16[1024,3072]{1,0:T(8,128)(2,1)S(1)} %shard_map.128.refs_0_.refs_1_.refs_2_.refs_3_) | copy-start | bytes 18874372
  50.2 2.1 %copy-start.10 = (f32[1024,640]{1,0:T(8,128)S(1)}, f32[1024,640]{1,0:T(8,128)}, u32[]{:S(2)}) copy-start(f32[1024,640]{1,0:T(8,128)} %copy-done.9) | copy-start | bytes 7864324
  50.3 20.3 %slice-start = ((s8[6291456]{0:T(1024)(128)(4,1)}), s8[4194304]{0:T(1024)(128)(4,1)S(1)}, s32[]{:S(2)}) async-start(s8[6291456]{0:T(1024)(128)(4,1)} %bitcast.68), calls=%async_computation.3 | async-start | bytes 8388608
  52.4 18.3 %slice-start.1 = ((s8[6291456]{0:T(1024)(128)(4,1)}), s8[2097152]{0:T(1024)(128)(4,1)S(1)}, s32[]{:S(2)}) async-start(s8[6291456]{0:T(1024)(128)(4,1)} %bitcast.68), calls=%async_computation.4 | async-start | bytes 4194304
  54.1 3.0 %copy-start.16 = (f32[128,1024]{1,0:T(8,128)S(1)}, f32[128,1024]{1,0:T(8,128)}, u32[]{:S(2)}) copy-start(f32[128,1024]{1,0:T(8,128)} %reduce-scatter.2.cloned.1.call-done) | copy-start | bytes 1572868
  54.1 16.5 %copy-start.14 = (bf16[1024,384]{1,0:T(8,128)(2,1)S(1)}, bf16[1024,384]{1,0:T(8,128)(2,1)}, u32[]{:S(2)}) copy-start(bf16[1024,384]{1,0:T(8,128)(2,1)} %copy-done.13) | copy-start | bytes 2359300
  54.4 31.1 %collective-permute-start.6 = (bf16[1024,640]{1,0:T(8,128)(2,1)S(1)}, bf16[1024,640]{1,0:T(8,128)(2,1)S(1)}, u32[]{:S(2)}, u32[]{:S(2)}) collective-permute-start(bf16[1024,640]{1,0:T(8,128)(2,1)S(1)} %pad_maximum_fusion.2), channel_id=1, source_target_pairs={{0,2},{1,3},{2,4},{3,5},{4,6},{5,7},{6,0},{7,1},{8,10},{9,11},{10,... | collective-permute-start | bytes 3932168 | tf_op jit(solution)/shard_map/ppermute | solution.py:52
  55.7 29.8 %collective-permute-start.7 = (bf16[1024,640]{1,0:T(8,128)(2,1)S(1)}, bf16[1024,640]{1,0:T(8,128)(2,1)S(1)}, u32[]{:S(2)}, u32[]{:S(2)}) collective-permute-start(bf16[1024,640]{1,0:T(8,128)(2,1)S(1)} %pad_maximum_fusion.3), channel_id=1, source_target_pairs={{0,6},{1,7},{2,0},{3,1},{4,2},{5,3},{6,4},{7,5},{8,14},{9,15},{10,... | collective-permute-start | bytes 3932168 | tf_op jit(solution)/shard_map/ppermute | solution.py:52
  57.2 12.2 %collective-permute-start.8 = (f32[128,1024]{1,0:T(8,128)S(1)}, f32[128,1024]{1,0:T(8,128)S(1)}, u32[]{:S(2)}, u32[]{:S(2)}) collective-permute-start(f32[128,1024]{1,0:T(8,128)S(1)} %copy-done.16), channel_id=1, source_target_pairs={{0,16},{16,0},{32,48},{48,32},{64,80},{80,64},{96,112},{112,96},{1... | collective-permute-start | bytes 1572872 | tf_op jit(solution)/shard_map/ppermute | solution.py:289
  58.4 39.1 %collective-permute-start.10 = (bf16[1536,384]{1,0:T(8,128)(2,1)}, bf16[1536,384]{1,0:T(8,128)(2,1)}, u32[]{:S(2)}, u32[]{:S(2)}) collective-permute-start(bf16[1536,384]{1,0:T(8,128)(2,1)} %fusion.2), channel_id=1, source_target_pairs={{0,8},{1,9},{2,10},{3,11},{4,12},{5,13},{6,14},{7,15},{8,0},{9,1},... | collective-permute-start | bytes 3538952 | tf_op jit(solution)/shard_map/ppermute | solution.py:52
  60.7 36.6 %collective-permute-start.11 = (bf16[256,384]{1,0:T(8,128)(2,1)}, bf16[256,384]{1,0:T(8,128)(2,1)}, u32[]{:S(2)}, u32[]{:S(2)}) collective-permute-start(bf16[256,384]{1,0:T(8,128)(2,1)} %get-tuple-element.115), channel_id=1, source_target_pairs={{0,2},{1,3},{2,4},{3,5},{4,6},{5,7},{6,0},{7,1},{8,10},{9,11},{10,... | collective-permute-start | bytes 589832 | tf_op jit(solution)/shard_map/ppermute | solution.py:52
  69.4 28.0 %collective-permute-start.12 = (bf16[256,384]{1,0:T(8,128)(2,1)}, bf16[256,384]{1,0:T(8,128)(2,1)}, u32[]{:S(2)}, u32[]{:S(2)}) collective-permute-start(bf16[256,384]{1,0:T(8,128)(2,1)} %get-tuple-element.116), channel_id=1, source_target_pairs={{0,6},{1,7},{2,0},{3,1},{4,2},{5,3},{6,4},{7,5},{8,14},{9,15},{10,... | collective-permute-start | bytes 589832 | tf_op jit(solution)/shard_map/ppermute | solution.py:52
  72.3 16.2 %copy-start.12 = (bf16[1024,640]{1,0:T(8,128)(2,1)S(1)}, bf16[1024,640]{1,0:T(8,128)(2,1)}, u32[]{:S(2)}) copy-start(bf16[1024,640]{1,0:T(8,128)(2,1)} %copy-done.11) | copy-start | bytes 3932164
  91.9 19.0 %collective-permute-start.9 = (bf16[512,640]{1,0:T(8,128)(2,1)}, bf16[512,640]{1,0:T(8,128)(2,1)}, u32[]{:S(2)}, u32[]{:S(2)}) collective-permute-start(bf16[512,640]{1,0:T(8,128)(2,1)} %fusion.24), channel_id=1, source_target_pairs={{0,8},{1,9},{2,10},{3,11},{4,12},{5,13},{6,14},{7,15},{8,0},{9,1},... | collective-permute-start | bytes 1966088 | tf_op jit(solution)/shard_map/ppermute | solution.py:52
  94.6 2.9 %copy-start.8 = (f32[1024,384]{1,0:T(8,128)S(1)}, f32[1024,384]{1,0:T(8,128)}, u32[]{:S(2)}) copy-start(f32[1024,384]{1,0:T(8,128)} %fusion.15) | copy-start | bytes 4718596
  94.6 2.9 %copy-start.15 = (f32[512,384]{1,0:T(8,128)S(1)}, f32[512,384]{1,0:T(8,128)}, u32[]{:S(2)}) copy-start(f32[512,384]{1,0:T(8,128)} %fusion.28) | copy-start | bytes 2359300
  101.0 11.5 %copy-start.5 = (f32[1,512,1024]{2,1,0:T(8,128)S(1)}, f32[1,512,1024]{2,1,0:T(8,128)}, u32[]{:S(2)}) copy-start(f32[1,512,1024]{2,1,0:T(8,128)} %param.11) | copy-start | bytes 6291460
  101.1 8.7 %collective-permute-start.13 = (bf16[512,384]{1,0:T(8,128)(2,1)S(1)}, bf16[512,384]{1,0:T(8,128)(2,1)S(1)}, u32[]{:S(2)}, u32[]{:S(2)}) collective-permute-start(bf16[512,384]{1,0:T(8,128)(2,1)S(1)} %pad_maximum_fusion.7), channel_id=1, source_target_pairs={{0,2},{1,3},{2,4},{3,5},{4,6},{5,7},{6,0},{7,1},{8,10},{9,11},{10,... | collective-permute-start | bytes 1179656 | tf_op jit(solution)/shard_map/ppermute | solution.py:52
  101.3 8.5 %collective-permute-start.14 = (bf16[512,384]{1,0:T(8,128)(2,1)S(1)}, bf16[512,384]{1,0:T(8,128)(2,1)S(1)}, u32[]{:S(2)}, u32[]{:S(2)}) collective-permute-start(bf16[512,384]{1,0:T(8,128)(2,1)S(1)} %pad_maximum_fusion.8), channel_id=1, source_target_pairs={{0,6},{1,7},{2,0},{3,1},{4,2},{5,3},{6,4},{7,5},{8,14},{9,15},{10,... | collective-permute-start | bytes 1179656 | tf_op jit(solution)/shard_map/ppermute | solution.py:52
  111.1 2.3 %copy-start.3 = (f32[1,512,1024]{2,1,0:T(8,128)S(1)}, f32[1,512,1024]{2,1,0:T(8,128)}, u32[]{:S(2)}) copy-start(f32[1,512,1024]{2,1,0:T(8,128)} %param.10) | copy-start | bytes 6291460
  116.0 23.2 %collective-permute-start.15 = (bf16[512,1024]{1,0:T(8,128)(2,1)}, bf16[512,1024]{1,0:T(8,128)(2,1)S(1)}, u32[]{:S(2)}, u32[]{:S(2)}) collective-permute-start(bf16[512,1024]{1,0:T(8,128)(2,1)} %get-tuple-element.141.refs_6_), channel_id=1, source_target_pairs={{0,2},{1,3},{2,4},{3,5},{4,6},{5,7},{6,0},{7,1},{8,10},{9,11},{10,... | collective-permute-start | bytes 3145736 | tf_op jit(solution)/shard_map/ppermute | solution.py:52
  116.0 23.2 %collective-permute-start.16 = (bf16[512,1024]{1,0:T(8,128)(2,1)}, bf16[512,1024]{1,0:T(8,128)(2,1)}, u32[]{:S(2)}, u32[]{:S(2)}) collective-permute-start(bf16[512,1024]{1,0:T(8,128)(2,1)} %get-tuple-element.141.refs_6_), channel_id=1, source_target_pairs={{0,6},{1,7},{2,0},{3,1},{4,2},{5,3},{6,4},{7,5},{8,14},{9,15},{10,... | collective-permute-start | bytes 3145736 | tf_op jit(solution)/shard_map/ppermute | solution.py:52
  118.6 23.0 %collective-permute-start.17 = (bf16[512,1024]{1,0:T(8,128)(2,1)}, bf16[512,1024]{1,0:T(8,128)(2,1)}, u32[]{:S(2)}, u32[]{:S(2)}) collective-permute-start(bf16[512,1024]{1,0:T(8,128)(2,1)} %get-tuple-element.141.refs_6_), channel_id=1, source_target_pairs={{0,8},{1,9},{2,10},{3,11},{4,12},{5,13},{6,14},{7,15},{8,0},{9,1},... | collective-permute-start | bytes 3145736 | tf_op jit(solution)/shard_map/ppermute | solution.py:52
  143.3 24.2 %collective-permute-start.18 = (bf16[1024,384]{1,0:T(8,128)(2,1)S(1)}, bf16[1024,384]{1,0:T(8,128)(2,1)S(1)}, u32[]{:S(2)}, u32[]{:S(2)}) collective-permute-start(bf16[1024,384]{1,0:T(8,128)(2,1)S(1)} %get-tuple-element.156), channel_id=1, source_target_pairs={{0,8},{1,9},{2,10},{3,11},{4,12},{5,13},{6,14},{7,15},{8,0},{9,1},... | collective-permute-start | bytes 2359304 | tf_op jit(solution)/shard_map/ppermute | solution.py:52
  143.4 24.1 %collective-permute-start.21 = (bf16[512,640]{1,0:T(8,128)(2,1)S(1)}, bf16[512,640]{1,0:T(8,128)(2,1)S(1)}, u32[]{:S(2)}, u32[]{:S(2)}) collective-permute-start(bf16[512,640]{1,0:T(8,128)(2,1)S(1)} %get-tuple-element.159), channel_id=1, source_target_pairs={{0,2},{1,3},{2,4},{3,5},{4,6},{5,7},{6,0},{7,1},{8,10},{9,11},{10,... | collective-permute-start | bytes 1966088 | tf_op jit(solution)/shard_map/ppermute | solution.py:52
  143.5 24.0 %collective-permute-start.22 = (bf16[512,640]{1,0:T(8,128)(2,1)S(1)}, bf16[512,640]{1,0:T(8,128)(2,1)S(1)}, u32[]{:S(2)}, u32[]{:S(2)}) collective-permute-start(bf16[512,640]{1,0:T(8,128)(2,1)S(1)} %get-tuple-element.159), channel_id=1, source_target_pairs={{0,6},{1,7},{2,0},{3,1},{4,2},{5,3},{6,4},{7,5},{8,14},{9,15},{10,... | collective-permute-start | bytes 1966088 | tf_op jit(solution)/shard_map/ppermute | solution.py:52
  146.1 21.3 %collective-permute-start.19 = (bf16[256,1024]{1,0:T(8,128)(2,1)S(1)}, bf16[256,1024]{1,0:T(8,128)(2,1)S(1)}, u32[]{:S(2)}, u32[]{:S(2)}) collective-permute-start(bf16[256,1024]{1,0:T(8,128)(2,1)S(1)} %get-tuple-element.157), channel_id=1, source_target_pairs={{0,2},{1,3},{2,4},{3,5},{4,6},{5,7},{6,0},{7,1},{8,10},{9,11},{10,... | collective-permute-start | bytes 1572872 | tf_op jit(solution)/shard_map/ppermute | solution.py:52
  146.2 21.3 %collective-permute-start.20 = (bf16[256,1024]{1,0:T(8,128)(2,1)S(1)}, bf16[256,1024]{1,0:T(8,128)(2,1)S(1)}, u32[]{:S(2)}, u32[]{:S(2)}) collective-permute-start(bf16[256,1024]{1,0:T(8,128)(2,1)S(1)} %get-tuple-element.158), channel_id=1, source_target_pairs={{0,6},{1,7},{2,0},{3,1},{4,2},{5,3},{6,4},{7,5},{8,14},{9,15},{10,... | collective-permute-start | bytes 1572872 | tf_op jit(solution)/shard_map/ppermute | solution.py:52
  148.8 2.8 %copy-start.1 = (bf16[1024,3072]{1,0:T(8,128)(2,1)S(1)}, bf16[1024,3072]{1,0:T(8,128)(2,1)}, u32[]{:S(2)}) copy-start(bf16[1024,3072]{1,0:T(8,128)(2,1)} %copy-done) | copy-start | bytes 18874372
  167.7 10.8 %collective-permute-start.23 = (bf16[512,384]{1,0:T(8,128)(2,1)S(1)}, bf16[512,384]{1,0:T(8,128)(2,1)S(1)}, u32[]{:S(2)}, u32[]{:S(2)}) collective-permute-start(bf16[512,384]{1,0:T(8,128)(2,1)S(1)} %pad_maximum_fusion.9), channel_id=1, source_target_pairs={{0,8},{1,9},{2,10},{3,11},{4,12},{5,13},{6,14},{7,15},{8,0},{9,1},... | collective-permute-start | bytes 1179656 | tf_op jit(solution)/shard_map/ppermute | solution.py:52
  170.6 7.9 %collective-permute-start.24 = (bf16[256,640]{1,0:T(8,128)(2,1)S(1)}, bf16[256,640]{1,0:T(8,128)(2,1)S(1)}, u32[]{:S(2)}, u32[]{:S(2)}) collective-permute-start(bf16[256,640]{1,0:T(8,128)(2,1)S(1)} %slice.154), channel_id=1, source_target_pairs={{0,2},{1,3},{2,4},{3,5},{4,6},{5,7},{6,0},{7,1},{8,10},{9,11},{10,... | collective-permute-start | bytes 983048 | tf_op jit(solution)/shard_map/ppermute | solution.py:52
  170.6 7.9 %collective-permute-start.25 = (bf16[256,640]{1,0:T(8,128)(2,1)S(1)}, bf16[256,640]{1,0:T(8,128)(2,1)S(1)}, u32[]{:S(2)}, u32[]{:S(2)}) collective-permute-start(bf16[256,640]{1,0:T(8,128)(2,1)S(1)} %slice.155), channel_id=1, source_target_pairs={{0,6},{1,7},{2,0},{3,1},{4,2},{5,3},{6,4},{7,5},{8,14},{9,15},{10,... | collective-permute-start | bytes 983048 | tf_op jit(solution)/shard_map/ppermute | solution.py:52
  179.7 11.2 %collective-permute-start.26 = (f32[512,1024]{1,0:T(8,128)S(1)}, f32[512,1024]{1,0:T(8,128)S(1)}, u32[]{:S(2)}, u32[]{:S(2)}) collective-permute-start(f32[512,1024]{1,0:T(8,128)S(1)} %shard_map.133), channel_id=1, source_target_pairs={{0,1},{1,0},{2,3},{3,2},{4,5},{5,4},{6,7},{7,6},{8,9},{9,8},{10,11... | collective-permute-start | bytes 6291464 | tf_op jit(solution)/shard_map/ppermute | solution.py:52
  (4 other events, 5.4 us)
Sparse Core Ops, SparseCore 0:
  13.6 32.7 reduce-scatter.1
  94.7 30.1 all-gather.1
